TPU v7x, 256 devices: a whole 4x4x8 slice. The times are simulated.
256 devices in a mesh: slab: 8 (over y, core), front: 32 (over z, x).
Axes of the slice: x: 4, y: 4, z: 8, core: 2. Of those that a mesh axis runs over, the one named last changes fastest.
Arguments:
- source: bfloat16 [8, 32, 2, 768, 128], P('slab', 'front'), may hold values from -6 to 6
- leaf_inverse: bfloat16 [8, 32, 2, 768, 768], P('slab', 'front'), may hold values from -0.15625 to 0.15625
- boundary_map: bfloat16 [8, 32, 2, 384, 768], P('slab', 'front'), may hold values from -0.15625 to 0.15625
- sep_inverse: bfloat16 [8, 96, 2, 384, 384], P('slab', 'front'), may hold values from -0.4375 to 0.4375
- owner_map: int32 [8, 64], P('slab'), may hold values from 0 to 31, as said below
- piece_count: int32 [8, 32], P('slab', 'front'), may hold values from 18 to 24, as said below
- piece_target: int32 [8, 32, 24], P('slab', 'front'), may hold values from 0 to 1535, as said below
Outputs:
- solution: bfloat16 [8, 32, 2, 768, 128], P('slab', 'front')
- trace: bfloat16 [8, 32, 24, 2, 16, 128], P('slab', 'front')
Inputs may be any that keep to these rules, and one draw needn't show every extreme that they name: `owner_map`: every owner holds 1 or 3 separators; a fraction 1 / 2 of the owners hold 3. `piece_count`: in every slab one leaf uses all its blocks. `piece_target`: entry j * 24 + q names part q of separator j. The used blocks of the leaves of one device name separators of one owner at most 2 times; in every slab some owner receives exactly 2 used blocks from every device.
All inputs are finite; a program needn't handle non-finite values.
Results may differ from a plain program's by a relative error of at most 0.025.
Values may be sent and summed in bfloat16 or wider, within the bound.
A program may use at most 128 MiB of HBM per device.

v0:
```python
import jax
import jax.numpy as jnp
from jax import lax
from jax.sharding import PartitionSpec as P


def shifted(block, axis, distance):
    devices = range(lax.axis_size(axis))
    route = [(i - distance, i) for i in devices if i - distance in devices]
    return lax.ppermute(block, axis, route)


def complex_product(form, left_real, left_imag, right_real, right_imag):
    real_part = jnp.einsum(
        form, left_real, right_real, preferred_element_type=jnp.float32
    ) - jnp.einsum(form, left_imag, right_imag, preferred_element_type=jnp.float32)
    imag_part = jnp.einsum(
        form, left_real, right_imag, preferred_element_type=jnp.float32
    ) + jnp.einsum(form, left_imag, right_real, preferred_element_type=jnp.float32)
    return (real_part, imag_part)


def body(source, leaf_inverse, boundary_map, sep_inverse, owner_map, piece_count, piece_target):
    leaf_rhs = source[0]
    inverse = leaf_inverse[0]
    coupling = boundary_map[0]
    sep_block = sep_inverse[0]
    owners = owner_map[0]
    counts = piece_count[0]
    targets = piece_target[0]
    leaves = leaf_rhs.shape[0]
    interior = leaf_rhs.shape[2]
    columns = leaf_rhs.shape[3]
    pieces = targets.shape[1]
    boundary = coupling.shape[2]
    piece_rows = boundary // pieces
    slots = sep_block.shape[0]
    sep_width = sep_block.shape[2]
    part_count = sep_width // piece_rows
    sep_count = owners.shape[0]
    front_size = lax.axis_size("front")
    slab_size = lax.axis_size("slab")
    total = leaves * pieces
    capacity = 2 * ((total // 2 + front_size - 1) // front_size)
    block_width = 2 * piece_rows * columns
    sep_ids = jnp.arange(sep_count, dtype=jnp.int32)
    earlier_sep = (owners[:, None] == owners[None, :]) & (sep_ids[:, None] > sep_ids[None, :])
    slot_of = jnp.sum(jnp.where(earlier_sep, 1, 0), axis=1).astype(jnp.int32)
    flat_target = targets.reshape(-1)
    sep_of = flat_target // part_count
    part_of = flat_target % part_count
    match_sep = sep_of[:, None] == sep_ids[None, :]
    destination = jnp.sum(jnp.where(match_sep, owners[None, :], 0), axis=1)
    position = jnp.sum(jnp.where(match_sep, slot_of[None, :], 0), axis=1) * part_count + part_of
    piece_ids = jnp.arange(total, dtype=jnp.int32)
    usable = (jnp.arange(pieces, dtype=jnp.int32)[None, :] < counts[:, None]).reshape(-1)
    before = (
        (destination[:, None] == destination[None, :])
        & usable[None, :]
        & (piece_ids[None, :] < piece_ids[:, None])
    )
    rank_within = jnp.sum(jnp.where(before, 1, 0), axis=1).astype(jnp.int32)
    slot_index = destination * capacity + rank_within
    buffer_ids = jnp.arange(front_size * capacity, dtype=jnp.int32)
    route = (buffer_ids[:, None] == slot_index[None, :]) & usable[None, :]
    weight = jnp.where(route, 1.0, 0.0).astype(jnp.bfloat16)
    tag = jnp.sum(jnp.where(route, position[None, :] + 1, 0), axis=1) - 1
    send_tag = tag.reshape(front_size, capacity)
    route_back = weight.T
    local_ids = jnp.arange(slots * part_count, dtype=jnp.int32)
    inv_real = inverse[:, 0]
    inv_imag = inverse[:, 1]
    near_real = inv_real[:, :, :boundary].reshape(leaves, interior, pieces, piece_rows)
    near_imag = inv_imag[:, :, :boundary].reshape(leaves, interior, pieces, piece_rows)
    couple_real = coupling[:, 0].reshape(leaves, pieces, piece_rows, interior)
    couple_imag = coupling[:, 1].reshape(leaves, pieces, piece_rows, interior)
    sep_real = sep_block[:, 0].reshape(slots, part_count, piece_rows, part_count, piece_rows)
    sep_imag = sep_block[:, 1].reshape(slots, part_count, piece_rows, part_count, piece_rows)

    def owner_values(incoming):
        base_real, base_imag = complex_product(
            "lnm,lmc->lnc", inv_real, inv_imag, leaf_rhs[:, 0], leaf_rhs[:, 1]
        )
        add_real, add_imag = complex_product(
            "lnpr,lprc->lnc", near_real, near_imag, incoming[:, :, 0], incoming[:, :, 1]
        )
        solution = jnp.stack([base_real + add_real, base_imag + add_imag], axis=1).astype(
            jnp.bfloat16
        )
        res_real, res_imag = complex_product(
            "lprm,lmc->lprc", couple_real, couple_imag, solution[:, 0], solution[:, 1]
        )
        resid = jnp.stack([res_real, res_imag], axis=2).astype(jnp.bfloat16)
        flat_blocks = resid.reshape(total, block_width)
        outgoing = jnp.dot(weight, flat_blocks, preferred_element_type=jnp.float32).astype(
            jnp.bfloat16
        )
        outgoing = outgoing.reshape(front_size, capacity, 2, piece_rows, columns)
        received, recv_tag = (
            lax.all_to_all(outgoing, "front", split_axis=0, concat_axis=0, tiled=True),
            lax.all_to_all(send_tag, "front", split_axis=0, concat_axis=0, tiled=True),
        )
        gather_weight = jnp.where(
            local_ids[:, None] == recv_tag.reshape(-1)[None, :], 1.0, 0.0
        ).astype(jnp.bfloat16)
        assembled = jnp.dot(
            gather_weight,
            received.reshape(front_size * capacity, block_width),
            preferred_element_type=jnp.float32,
        ).astype(jnp.bfloat16)
        assembled = assembled.reshape(slots, part_count, 2, piece_rows, columns)
        val_real, val_imag = complex_product(
            "kabpr,kprc->kabc", sep_real, sep_imag, assembled[:, :, 0], assembled[:, :, 1]
        )
        values = jnp.stack([val_real, val_imag], axis=2).astype(jnp.bfloat16)
        returned = jnp.dot(
            gather_weight.T,
            values.reshape(slots * part_count, block_width),
            preferred_element_type=jnp.float32,
        ).astype(jnp.bfloat16)
        returned = returned.reshape(front_size, capacity, 2, piece_rows, columns)
        return (solution, returned)

    def own_trace(returned):
        answers = lax.all_to_all(returned, "front", split_axis=0, concat_axis=0, tiled=True)
        trace_out = jnp.dot(
            route_back,
            answers.reshape(front_size * capacity, block_width),
            preferred_element_type=jnp.float32,
        ).astype(jnp.bfloat16)
        return trace_out.reshape(leaves, pieces, 2, piece_rows, columns)

    empty_trace = jnp.zeros((leaves, pieces, 2, piece_rows, columns), jnp.bfloat16)

    def slab_step(incoming):
        solution, returned = owner_values(incoming)
        return (solution, own_trace(returned))

    first_state = slab_step(empty_trace)

    def advance(step_index, carried):
        incoming = shifted(carried[1], "slab", 1)
        return slab_step(incoming)

    solution, trace_out = lax.fori_loop(0, slab_size - 1, advance, first_state)
    return (solution[None], trace_out[None])


def solution(mesh):
    placed = (
        P("slab", "front", None, None, None),
        P("slab", "front", None, None, None),
        P("slab", "front", None, None, None),
        P("slab", "front", None, None, None),
        P("slab", None),
        P("slab", "front"),
        P("slab", "front", None),
    )
    return jax.shard_map(
        body,
        mesh=mesh,
        in_specs=placed,
        out_specs=(
            P("slab", "front", None, None, None),
            P("slab", "front", None, None, None, None),
        ),
        check_vma=False,
    )
```

profile of v0, /device:TPU:8, one launch (start us, length us, event | category | flops | bytes accessed | tf_op | source)
XLA Modules:
  0.0 562.8 jit_solution(14156290141849751092)
XLA Ops:
  16.6 11.3 %all-to-all-start.2 = ((s32[32,1,2]{2,1,0:T(1,128)}), s32[32,1,2]{2,1,0:T(1,128)S(1)}, u32[]{:S(2)}, u32[]{:S(2)}) async-start(s32[32,1,2]{2,1,0:T(1,128)} %bitcast.25), calls=%async_computation.2 | async-start | bytes 32768 | tf_op jit(solution)/shard_map/all_to_all | solution.py:101
  29.3 8.5 %all-to-all-done.2 = s32[32,1,2]{2,1,0:T(1,128)S(1)} async-done(((s32[32,1,2]{2,1,0:T(1,128)}), s32[32,1,2]{2,1,0:T(1,128)S(1)}, u32[]{:S(2)}, u32[]{:S(2)}) %all-to-all-start.2) | async-done | bytes 288 | tf_op jit(solution)/shard_map/all_to_all | solution.py:101
  43.4 6.6 %reshape_squeeze.13 = bf16[3,24,16,24,16]{4,3,2,1,0:T(8,128)(2,1)} reshape(bf16[3,1,384,384]{3,2,1,0:T(8,128)(2,1)S(1)} %get-tuple-element.339) | data formatting | bytes 1769472 | tf_op jit(solution)/shard_map/reshape;squeeze | solution.py:77
  50.0 8.5 %copy.99 = bf16[3,24,16,24,16]{3,1,4,2,0:T(8,128)(2,1)} copy(bf16[3,24,16,24,16]{4,3,2,1,0:T(8,128)(2,1)} %reshape_squeeze.13) | data formatting | bytes 1769472 | tf_op jit(solution)/shard_map/reshape;squeeze | solution.py:77
  58.5 6.6 %reshape_squeeze.14 = bf16[3,24,16,24,16]{4,3,2,1,0:T(8,128)(2,1)} reshape(bf16[3,1,384,384]{3,2,1,0:T(8,128)(2,1)S(1)} %get-tuple-element.340) | data formatting | bytes 1769472 | tf_op jit(solution)/shard_map/reshape;squeeze | solution.py:78
  65.1 8.6 %copy.101 = bf16[3,24,16,24,16]{3,1,4,2,0:T(8,128)(2,1)} copy(bf16[3,24,16,24,16]{4,3,2,1,0:T(8,128)(2,1)} %reshape_squeeze.14) | data formatting | bytes 1769472 | tf_op jit(solution)/shard_map/reshape;squeeze | solution.py:78
  86.5 9.6 %all-to-all-start.4 = ((bf16[32,2,2,16,128]{4,3,2,1,0:T(8,128)(2,1)}), bf16[32,2,2,16,128]{4,3,2,1,0:T(8,128)(2,1)S(1)}, u32[]{:S(2)}, u32[]{:S(2)}) async-start(bf16[32,2,2,16,128]{4,3,2,1,0:T(8,128)(2,1)} %bitcast.141), calls=%async_computation.4 | async-start | bytes 1048576 | tf_op jit(solution)/shard_map/all_to_all | solution.py:125
  101.5 10.8 %all-to-all-done.4 = bf16[32,2,2,16,128]{4,3,2,1,0:T(8,128)(2,1)S(1)} async-done(((bf16[32,2,2,16,128]{4,3,2,1,0:T(8,128)(2,1)}), bf16[32,2,2,16,128]{4,3,2,1,0:T(8,128)(2,1)S(1)}, u32[]{:S(2)}, u32[]{:S(2)}) %all-to-all-start.4) | async-done | bytes 524320 | tf_op jit(solution)/shard_map/all_to_all | solution.py:125
  113.0 449.1 %while.17 = (s32[]{:T(128)}, bf16[1,2,768,128]{3,2,1,0:T(8,128)(2,1)}, bf16[1,24,2,16,128]{4,3,2,1,0:T(8,128)(2,1)S(1)}, bf16[1,768,24,16]{1,2,3,0:T(8,128)(2,1)...) while((s32[]{:T(128)}, ...), condition=%wide.wide.region_6.7_spmd.clone.clone, body=%wide.wide.region_5.6_spmd.clone.clone.sunk | while | flops 1160551424 | bytes 74189552 | solution.py:145
  126.2 21.4 %all_to_all.42 = bf16[32,2,2,16,128]{4,3,2,1,0:T(8,128)(2,1)S(1)} all-to-all(bf16[32,2,2,16,128]{4,3,2,1,0:T(8,128)(2,1)S(1)} %bitcast.481), channel_id=1, replica_groups=mesh['slab'=8,'front'=32] {'front'}, dimensions={0} | all-to-all | bytes 1048576 | tf_op jit(solution)/shard_map/while/body/eval_jaxpr/all_to_all | solution.py:100
  164.5 16.2 %all-to-all-done.1 = bf16[32,2,2,16,128]{4,3,2,1,0:T(8,128)(2,1)S(1)} async-done(((bf16[32,2,2,16,128]{4,3,2,1,0:T(8,128)(2,1)}), bf16[32,2,2,16,128]{4,3,2,1,0:T(8,128)(2,1)S(1)}, u32[]{:S(2)}, u32[]{:S(2)}) %all-to-all-start.1) | async-done | bytes 524320 | tf_op jit(solution)/shard_map/while/body/eval_jaxpr/all_to_all | solution.py:125
  194.3 21.2 %all_to_all.42 = bf16[32,2,2,16,128]{4,3,2,1,0:T(8,128)(2,1)S(1)} all-to-all(bf16[32,2,2,16,128]{4,3,2,1,0:T(8,128)(2,1)S(1)} %bitcast.481), channel_id=1, replica_groups=mesh['slab'=8,'front'=32] {'front'}, dimensions={0} | all-to-all | bytes 1048576 | tf_op jit(solution)/shard_map/while/body/eval_jaxpr/all_to_all | solution.py:100
  232.3 16.1 %all-to-all-done.1 = bf16[32,2,2,16,128]{4,3,2,1,0:T(8,128)(2,1)S(1)} async-done(((bf16[32,2,2,16,128]{4,3,2,1,0:T(8,128)(2,1)}), bf16[32,2,2,16,128]{4,3,2,1,0:T(8,128)(2,1)S(1)}, u32[]{:S(2)}, u32[]{:S(2)}) %all-to-all-start.1) | async-done | bytes 524320 | tf_op jit(solution)/shard_map/while/body/eval_jaxpr/all_to_all | solution.py:125
  262.0 19.3 %all_to_all.42 = bf16[32,2,2,16,128]{4,3,2,1,0:T(8,128)(2,1)S(1)} all-to-all(bf16[32,2,2,16,128]{4,3,2,1,0:T(8,128)(2,1)S(1)} %bitcast.481), channel_id=1, replica_groups=mesh['slab'=8,'front'=32] {'front'}, dimensions={0} | all-to-all | bytes 1048576 | tf_op jit(solution)/shard_map/while/body/eval_jaxpr/all_to_all | solution.py:100
  297.6 13.8 %all-to-all-done.1 = bf16[32,2,2,16,128]{4,3,2,1,0:T(8,128)(2,1)S(1)} async-done(((bf16[32,2,2,16,128]{4,3,2,1,0:T(8,128)(2,1)}), bf16[32,2,2,16,128]{4,3,2,1,0:T(8,128)(2,1)S(1)}, u32[]{:S(2)}, u32[]{:S(2)}) %all-to-all-start.1) | async-done | bytes 524320 | tf_op jit(solution)/shard_map/while/body/eval_jaxpr/all_to_all | solution.py:125
  314.0 5.1 collective-permute-done
  325.0 18.8 %all_to_all.42 = bf16[32,2,2,16,128]{4,3,2,1,0:T(8,128)(2,1)S(1)} all-to-all(bf16[32,2,2,16,128]{4,3,2,1,0:T(8,128)(2,1)S(1)} %bitcast.481), channel_id=1, replica_groups=mesh['slab'=8,'front'=32] {'front'}, dimensions={0} | all-to-all | bytes 1048576 | tf_op jit(solution)/shard_map/while/body/eval_jaxpr/all_to_all | solution.py:100
  360.1 13.8 %all-to-all-done.1 = bf16[32,2,2,16,128]{4,3,2,1,0:T(8,128)(2,1)S(1)} async-done(((bf16[32,2,2,16,128]{4,3,2,1,0:T(8,128)(2,1)}), bf16[32,2,2,16,128]{4,3,2,1,0:T(8,128)(2,1)S(1)}, u32[]{:S(2)}, u32[]{:S(2)}) %all-to-all-start.1) | async-done | bytes 524320 | tf_op jit(solution)/shard_map/while/body/eval_jaxpr/all_to_all | solution.py:125
  387.5 18.8 %all_to_all.42 = bf16[32,2,2,16,128]{4,3,2,1,0:T(8,128)(2,1)S(1)} all-to-all(bf16[32,2,2,16,128]{4,3,2,1,0:T(8,128)(2,1)S(1)} %bitcast.481), channel_id=1, replica_groups=mesh['slab'=8,'front'=32] {'front'}, dimensions={0} | all-to-all | bytes 1048576 | tf_op jit(solution)/shard_map/while/body/eval_jaxpr/all_to_all | solution.py:100
  422.6 13.8 %all-to-all-done.1 = bf16[32,2,2,16,128]{4,3,2,1,0:T(8,128)(2,1)S(1)} async-done(((bf16[32,2,2,16,128]{4,3,2,1,0:T(8,128)(2,1)}), bf16[32,2,2,16,128]{4,3,2,1,0:T(8,128)(2,1)S(1)}, u32[]{:S(2)}, u32[]{:S(2)}) %all-to-all-start.1) | async-done | bytes 524320 | tf_op jit(solution)/shard_map/while/body/eval_jaxpr/all_to_all | solution.py:125
  450.1 18.8 %all_to_all.42 = bf16[32,2,2,16,128]{4,3,2,1,0:T(8,128)(2,1)S(1)} all-to-all(bf16[32,2,2,16,128]{4,3,2,1,0:T(8,128)(2,1)S(1)} %bitcast.481), channel_id=1, replica_groups=mesh['slab'=8,'front'=32] {'front'}, dimensions={0} | all-to-all | bytes 1048576 | tf_op jit(solution)/shard_map/while/body/eval_jaxpr/all_to_all | solution.py:100
  485.2 13.8 %all-to-all-done.1 = bf16[32,2,2,16,128]{4,3,2,1,0:T(8,128)(2,1)S(1)} async-done(((bf16[32,2,2,16,128]{4,3,2,1,0:T(8,128)(2,1)}), bf16[32,2,2,16,128]{4,3,2,1,0:T(8,128)(2,1)S(1)}, u32[]{:S(2)}, u32[]{:S(2)}) %all-to-all-start.1) | async-done | bytes 524320 | tf_op jit(solution)/shard_map/while/body/eval_jaxpr/all_to_all | solution.py:125
  512.6 18.8 %all_to_all.42 = bf16[32,2,2,16,128]{4,3,2,1,0:T(8,128)(2,1)S(1)} all-to-all(bf16[32,2,2,16,128]{4,3,2,1,0:T(8,128)(2,1)S(1)} %bitcast.481), channel_id=1, replica_groups=mesh['slab'=8,'front'=32] {'front'}, dimensions={0} | all-to-all | bytes 1048576 | tf_op jit(solution)/shard_map/while/body/eval_jaxpr/all_to_all | solution.py:100
  547.7 13.8 %all-to-all-done.1 = bf16[32,2,2,16,128]{4,3,2,1,0:T(8,128)(2,1)S(1)} async-done(((bf16[32,2,2,16,128]{4,3,2,1,0:T(8,128)(2,1)}), bf16[32,2,2,16,128]{4,3,2,1,0:T(8,128)(2,1)S(1)}, u32[]{:S(2)}, u32[]{:S(2)}) %all-to-all-start.1) | async-done | bytes 524320 | tf_op jit(solution)/shard_map/while/body/eval_jaxpr/all_to_all | solution.py:125
  (529 shorter events, 244.1 us)
Async XLA Ops:
  16.6 21.1 %all-to-all-start.2 = ((s32[32,1,2]{2,1,0:T(1,128)}), s32[32,1,2]{2,1,0:T(1,128)S(1)}, u32[]{:S(2)}, u32[]{:S(2)}) async-start(s32[32,1,2]{2,1,0:T(1,128)} %bitcast.25), calls=%async_computation.2 | async-start | bytes 32768 | tf_op jit(solution)/shard_map/all_to_all | solution.py:101
  37.7 63.2 %copy-start.26 = (s32[32,1,2]{2,1,0:T(1,128)}, s32[32,1,2]{2,1,0:T(1,128)S(1)}, u32[]{:S(2)}) copy-start(s32[32,1,2]{2,1,0:T(1,128)S(1)} %all-to-all-done.2) | copy-start | bytes 772
  37.7 37.3 %all-to-all-start.3 = ((bf16[32,2,2,16,128]{4,3,2,1,0:T(8,128)(2,1)}), bf16[32,2,2,16,128]{4,3,2,1,0:T(8,128)(2,1)S(1)}, u32[]{:S(2)}, u32[]{:S(2)}) async-start(bf16[32,2,2,16,128]{4,3,2,1,0:T(8,128)(2,1)} %bitcast.131), calls=%async_computation.3 | async-start | bytes 1048576 | tf_op jit(solution)/shard_map/all_to_all | solution.py:100
  86.5 25.9 %all-to-all-start.4 = ((bf16[32,2,2,16,128]{4,3,2,1,0:T(8,128)(2,1)}), bf16[32,2,2,16,128]{4,3,2,1,0:T(8,128)(2,1)S(1)}, u32[]{:S(2)}, u32[]{:S(2)}) async-start(bf16[32,2,2,16,128]{4,3,2,1,0:T(8,128)(2,1)} %bitcast.141), calls=%async_computation.4 | async-start | bytes 1048576 | tf_op jit(solution)/shard_map/all_to_all | solution.py:125
  113.3 7.0 %collective-permute-start = (bf16[1,24,2,16,128]{4,1,3,2,0:T(8,128)(2,1)S(1)}, bf16[1,24,2,16,128]{4,1,3,2,0:T(8,128)(2,1)S(1)}, u32[]{:S(2)}, u32[]{:S(2)}) collective-permute-start(bf16[1,24,2,16,128]{4,1,3,2,0:T(8,128)(2,1)S(1)} %copy.192), channel_id=1, source_target_pairs={{0,32},{32,64},{64,96},{96,128},{128,160},{160,192},{192,224},{1,3... | collective-permute-start | bytes 589832 | tf_op jit(solution)/shard_map/while/body/eval_jaxpr/ppermute | solution.py:10
  125.7 26.8 %slice-start.4 = ((s8[4718592]{0:T(1024)(128)(4,1)}), s8[524288]{0:T(1024)(128)(4,1)S(1)}, s32[]{:S(2)}) async-start(s8[4718592]{0:T(1024)(128)(4,1)} %bitcast.478), calls=%async_computation.9 | async-start | bytes 1048576 | tf_op jit(solution)/shard_map/while
  159.1 21.6 %all-to-all-start.1 = ((bf16[32,2,2,16,128]{4,3,2,1,0:T(8,128)(2,1)}), bf16[32,2,2,16,128]{4,3,2,1,0:T(8,128)(2,1)S(1)}, u32[]{:S(2)}, u32[]{:S(2)}) async-start(bf16[32,2,2,16,128]{4,3,2,1,0:T(8,128)(2,1)} %bitcast.471), calls=%async_computation.1 | async-start | bytes 1048576 | tf_op jit(solution)/shard_map/while/body/eval_jaxpr/all_to_all | solution.py:125
  181.3 7.0 %collective-permute-start = (bf16[1,24,2,16,128]{4,1,3,2,0:T(8,128)(2,1)S(1)}, bf16[1,24,2,16,128]{4,1,3,2,0:T(8,128)(2,1)S(1)}, u32[]{:S(2)}, u32[]{:S(2)}) collective-permute-start(bf16[1,24,2,16,128]{4,1,3,2,0:T(8,128)(2,1)S(1)} %copy.192), channel_id=1, source_target_pairs={{0,32},{32,64},{64,96},{96,128},{128,160},{160,192},{192,224},{1,3... | collective-permute-start | bytes 589832 | tf_op jit(solution)/shard_map/while/body/eval_jaxpr/ppermute | solution.py:10
  193.8 26.6 %slice-start.4 = ((s8[4718592]{0:T(1024)(128)(4,1)}), s8[524288]{0:T(1024)(128)(4,1)S(1)}, s32[]{:S(2)}) async-start(s8[4718592]{0:T(1024)(128)(4,1)} %bitcast.478), calls=%async_computation.9 | async-start | bytes 1048576 | tf_op jit(solution)/shard_map/while
  227.0 21.4 %all-to-all-start.1 = ((bf16[32,2,2,16,128]{4,3,2,1,0:T(8,128)(2,1)}), bf16[32,2,2,16,128]{4,3,2,1,0:T(8,128)(2,1)S(1)}, u32[]{:S(2)}, u32[]{:S(2)}) async-start(bf16[32,2,2,16,128]{4,3,2,1,0:T(8,128)(2,1)} %bitcast.471), calls=%async_computation.1 | async-start | bytes 1048576 | tf_op jit(solution)/shard_map/while/body/eval_jaxpr/all_to_all | solution.py:125
  249.1 7.0 %collective-permute-start = (bf16[1,24,2,16,128]{4,1,3,2,0:T(8,128)(2,1)S(1)}, bf16[1,24,2,16,128]{4,1,3,2,0:T(8,128)(2,1)S(1)}, u32[]{:S(2)}, u32[]{:S(2)}) collective-permute-start(bf16[1,24,2,16,128]{4,1,3,2,0:T(8,128)(2,1)S(1)} %copy.192), channel_id=1, source_target_pairs={{0,32},{32,64},{64,96},{96,128},{128,160},{160,192},{192,224},{1,3... | collective-permute-start | bytes 589832 | tf_op jit(solution)/shard_map/while/body/eval_jaxpr/ppermute | solution.py:10
  261.5 24.7 %slice-start.4 = ((s8[4718592]{0:T(1024)(128)(4,1)}), s8[524288]{0:T(1024)(128)(4,1)S(1)}, s32[]{:S(2)}) async-start(s8[4718592]{0:T(1024)(128)(4,1)} %bitcast.478), calls=%async_computation.9 | async-start | bytes 1048576 | tf_op jit(solution)/shard_map/while
  292.8 18.6 %all-to-all-start.1 = ((bf16[32,2,2,16,128]{4,3,2,1,0:T(8,128)(2,1)}), bf16[32,2,2,16,128]{4,3,2,1,0:T(8,128)(2,1)S(1)}, u32[]{:S(2)}, u32[]{:S(2)}) async-start(bf16[32,2,2,16,128]{4,3,2,1,0:T(8,128)(2,1)} %bitcast.471), calls=%async_computation.1 | async-start | bytes 1048576 | tf_op jit(solution)/shard_map/while/body/eval_jaxpr/all_to_all | solution.py:125
  312.0 7.0 %collective-permute-start = (bf16[1,24,2,16,128]{4,1,3,2,0:T(8,128)(2,1)S(1)}, bf16[1,24,2,16,128]{4,1,3,2,0:T(8,128)(2,1)S(1)}, u32[]{:S(2)}, u32[]{:S(2)}) collective-permute-start(bf16[1,24,2,16,128]{4,1,3,2,0:T(8,128)(2,1)S(1)} %copy.192), channel_id=1, source_target_pairs={{0,32},{32,64},{64,96},{96,128},{128,160},{160,192},{192,224},{1,3... | collective-permute-start | bytes 589832 | tf_op jit(solution)/shard_map/while/body/eval_jaxpr/ppermute | solution.py:10
  324.5 24.2 %slice-start.4 = ((s8[4718592]{0:T(1024)(128)(4,1)}), s8[524288]{0:T(1024)(128)(4,1)S(1)}, s32[]{:S(2)}) async-start(s8[4718592]{0:T(1024)(128)(4,1)} %bitcast.478), calls=%async_computation.9 | async-start | bytes 1048576 | tf_op jit(solution)/shard_map/while
  355.3 18.6 %all-to-all-start.1 = ((bf16[32,2,2,16,128]{4,3,2,1,0:T(8,128)(2,1)}), bf16[32,2,2,16,128]{4,3,2,1,0:T(8,128)(2,1)S(1)}, u32[]{:S(2)}, u32[]{:S(2)}) async-start(bf16[32,2,2,16,128]{4,3,2,1,0:T(8,128)(2,1)} %bitcast.471), calls=%async_computation.1 | async-start | bytes 1048576 | tf_op jit(solution)/shard_map/while/body/eval_jaxpr/all_to_all | solution.py:125
  374.6 7.0 %collective-permute-start = (bf16[1,24,2,16,128]{4,1,3,2,0:T(8,128)(2,1)S(1)}, bf16[1,24,2,16,128]{4,1,3,2,0:T(8,128)(2,1)S(1)}, u32[]{:S(2)}, u32[]{:S(2)}) collective-permute-start(bf16[1,24,2,16,128]{4,1,3,2,0:T(8,128)(2,1)S(1)} %copy.192), channel_id=1, source_target_pairs={{0,32},{32,64},{64,96},{96,128},{128,160},{160,192},{192,224},{1,3... | collective-permute-start | bytes 589832 | tf_op jit(solution)/shard_map/while/body/eval_jaxpr/ppermute | solution.py:10
  387.0 24.2 %slice-start.4 = ((s8[4718592]{0:T(1024)(128)(4,1)}), s8[524288]{0:T(1024)(128)(4,1)S(1)}, s32[]{:S(2)}) async-start(s8[4718592]{0:T(1024)(128)(4,1)} %bitcast.478), calls=%async_computation.9 | async-start | bytes 1048576 | tf_op jit(solution)/shard_map/while
  417.8 18.6 %all-to-all-start.1 = ((bf16[32,2,2,16,128]{4,3,2,1,0:T(8,128)(2,1)}), bf16[32,2,2,16,128]{4,3,2,1,0:T(8,128)(2,1)S(1)}, u32[]{:S(2)}, u32[]{:S(2)}) async-start(bf16[32,2,2,16,128]{4,3,2,1,0:T(8,128)(2,1)} %bitcast.471), calls=%async_computation.1 | async-start | bytes 1048576 | tf_op jit(solution)/shard_map/while/body/eval_jaxpr/all_to_all | solution.py:125
  437.1 7.0 %collective-permute-start = (bf16[1,24,2,16,128]{4,1,3,2,0:T(8,128)(2,1)S(1)}, bf16[1,24,2,16,128]{4,1,3,2,0:T(8,128)(2,1)S(1)}, u32[]{:S(2)}, u32[]{:S(2)}) collective-permute-start(bf16[1,24,2,16,128]{4,1,3,2,0:T(8,128)(2,1)S(1)} %copy.192), channel_id=1, source_target_pairs={{0,32},{32,64},{64,96},{96,128},{128,160},{160,192},{192,224},{1,3... | collective-permute-start | bytes 589832 | tf_op jit(solution)/shard_map/while/body/eval_jaxpr/ppermute | solution.py:10
  449.5 24.2 %slice-start.4 = ((s8[4718592]{0:T(1024)(128)(4,1)}), s8[524288]{0:T(1024)(128)(4,1)S(1)}, s32[]{:S(2)}) async-start(s8[4718592]{0:T(1024)(128)(4,1)} %bitcast.478), calls=%async_computation.9 | async-start | bytes 1048576 | tf_op jit(solution)/shard_map/while
  480.4 18.6 %all-to-all-start.1 = ((bf16[32,2,2,16,128]{4,3,2,1,0:T(8,128)(2,1)}), bf16[32,2,2,16,128]{4,3,2,1,0:T(8,128)(2,1)S(1)}, u32[]{:S(2)}, u32[]{:S(2)}) async-start(bf16[32,2,2,16,128]{4,3,2,1,0:T(8,128)(2,1)} %bitcast.471), calls=%async_computation.1 | async-start | bytes 1048576 | tf_op jit(solution)/shard_map/while/body/eval_jaxpr/all_to_all | solution.py:125
  499.7 7.0 %collective-permute-start = (bf16[1,24,2,16,128]{4,1,3,2,0:T(8,128)(2,1)S(1)}, bf16[1,24,2,16,128]{4,1,3,2,0:T(8,128)(2,1)S(1)}, u32[]{:S(2)}, u32[]{:S(2)}) collective-permute-start(bf16[1,24,2,16,128]{4,1,3,2,0:T(8,128)(2,1)S(1)} %copy.192), channel_id=1, source_target_pairs={{0,32},{32,64},{64,96},{96,128},{128,160},{160,192},{192,224},{1,3... | collective-permute-start | bytes 589832 | tf_op jit(solution)/shard_map/while/body/eval_jaxpr/ppermute | solution.py:10
  542.9 18.6 %all-to-all-start.1 = ((bf16[32,2,2,16,128]{4,3,2,1,0:T(8,128)(2,1)}), bf16[32,2,2,16,128]{4,3,2,1,0:T(8,128)(2,1)S(1)}, u32[]{:S(2)}, u32[]{:S(2)}) async-start(bf16[32,2,2,16,128]{4,3,2,1,0:T(8,128)(2,1)} %bitcast.471), calls=%async_computation.1 | async-start | bytes 1048576 | tf_op jit(solution)/shard_map/while/body/eval_jaxpr/all_to_all | solution.py:125
  (103 other events, 1076.5 us)
where the time goes:
time: 566 us; the launch traced here: 563 us
  waiting for transfers between devices  156 us (28%)
  blocking collectives  137 us (24%)
  matrix products  122 us (22%)
  starting transfers between devices  67.6 us (12%)
  local copies, waits for them, and re-layouts  67.1 us (12%)
  other arithmetic  8.23 us (1%)
    all_to_all x7, blocking collectives, owner_values(): lax.all_to_all(outgoing, 'front', split_axis=0, concat_axis=0, tiled=True)  137 us
    all_to_all x8, waiting for transfers between devices, own_trace(): lax.all_to_all(returned, 'front', split_axis=0, concat_axis=0, tiled=True)  112 us
    all_to_all x8, starting transfers between devices, own_trace(): lax.all_to_all(returned, 'front', split_axis=0, concat_axis=0, tiled=True)  38.8 us
    dot_general x24, matrix products, complex_product(): jnp.einsum(form, left_imag, right_real, preferred_element_type=jnp.float32)  38.4 us
    ppermute x7, waiting for transfers between devices, shifted(): return lax.ppermute(block, axis, route)  35.4 us
    dot_general x24, matrix products, complex_product(): jnp.einsum(form, left_real, right_imag, preferred_element_type=jnp.float32)  27.3 us
    dot_general x25, matrix products, complex_product(): jnp.einsum(form, left_imag, right_imag, preferred_element_type=jnp.float32)  27.1 us
    dot_general x25, matrix products, complex_product(): jnp.einsum(form, left_real, right_real, preferred_element_type=jnp.float32)  19.8 us
  transfers between devices with their start and end apart: 17, of which 16 were waited for; matrix products, arithmetic and copies ran while one was open for 8% of the time, Pallas kernels for 0%

commit v1 on v0

v1 whole, which is shorter than its diff:
```python
import functools

import jax
import jax.numpy as jnp
from jax import lax
from jax.experimental import pallas as pl
from jax.experimental.pallas import tpu as pltpu
from jax.sharding import PartitionSpec as P

MESH = pl.DeviceIdType.MESH
BF16 = jnp.bfloat16
F32 = jnp.float32
LANES = 128


def mm(a, b):
    return jnp.dot(a, b, preferred_element_type=F32)


def sweep_kernel(
    slabs,
    fronts,
    ring,
    src_ref,
    inv_hbm,
    cpl_hbm,
    sep_hbm,
    tab_ref,
    tab_smem,
    sol_ref,
    trace_ref,
    leaf2,
    cpl2,
    sep2,
    comp2,
    xs,
    xb,
    xin,
    xsep,
    base,
    resid0,
    rblk,
    inc,
    out_a,
    recv_a,
    run,
    vals,
    out_b,
    recv_b,
    recv_t,
    home,
    tag_recv,
    tab_recv,
    own_tab,
    own_smem,
    prev_smem,
    load_sem,
    sep_sem,
    tag_send,
    tag_arrive,
    prev_send,
    prev_arrive,
    a_send,
    a_arrive,
    b_send,
    b_arrive,
    t_arrive,
    home_send,
    home_arrive,
    smem_sem,
):
    s = lax.axis_index("slab")
    f = lax.axis_index("front")
    last = slabs - 1
    interior, cols = src_ref.shape[1], src_ref.shape[2]
    bnd = cpl2.shape[0]
    slots, sepw = sep2.shape[0], sep2.shape[1]
    pieces = inc.shape[0]
    rows = inc.shape[2]
    parts = sepw // rows
    positions = slots * parts
    cap = 2 * fronts
    halves = interior // bnd
    depth = fronts // ring

    def peer(i):
        j, k = i // ring, i % ring
        dz = depth // 2 + (1 - 2 * (j % 2)) * ((j + 1) // 2)
        dx = ring // 2 + (1 - 2 * (k % 2)) * ((k + 1) // 2)
        return (f // ring + dz) % depth * ring + (f % ring + dx) % ring

    barrier = pltpu.get_barrier_semaphore()

    def greet(slab_to, count):
        def one(i, carry):
            pl.semaphore_signal(
                barrier, inc=1, device_id=(slab_to, peer(i)), device_id_type=MESH
            )
            return carry

        lax.fori_loop(0, count, one, 0)

    greet(s, fronts - 1)

    @pl.when(s > 0)
    def _():
        greet(s - 1, fronts)

    @pl.when(s < last)
    def _():
        pl.semaphore_signal(barrier, inc=1, device_id=(s + 1, f), device_id_type=MESH)

    loads = []
    for h in range(halves):
        for c in range(2):
            at = (2 * h + c) * bnd
            loads.append(
                pltpu.make_async_copy(
                    inv_hbm.at[c, :, pl.ds(h * bnd, bnd)],
                    leaf2.at[:, pl.ds(at, bnd)],
                    load_sem.at[2 * h + c],
                )
            )
    for c in range(2):
        loads.append(
            pltpu.make_async_copy(
                cpl_hbm.at[c],
                cpl2.at[:, pl.ds(c * interior, interior)],
                load_sem.at[2 * halves + c],
            )
        )
    sep_loads = []
    for m in range(slots):
        for c in range(2):
            sep_loads.append(
                pltpu.make_async_copy(
                    sep_hbm.at[m, c],
                    sep2.at[m, :, pl.ds(c * sepw, sepw)],
                    sep_sem.at[2 * m + c],
                )
            )
    for copy in loads + sep_loads:
        copy.start()

    zero_block = jnp.zeros((2, rows, cols), BF16)
    rblk[pieces] = zero_block
    vals[positions] = zero_block
    run[cap] = jnp.zeros((2, rows, cols), F32)
    recv_b[cap] = zero_block
    recv_t[cap] = zero_block

    for h in range(halves):
        real = src_ref[0, pl.ds(h * bnd, bnd), :]
        imag = src_ref[1, pl.ds(h * bnd, bnd), :]
        top, low = pl.ds(2 * h * bnd, bnd), pl.ds((2 * h + 1) * bnd, bnd)
        xs[top, pl.ds(0, cols)] = real
        xs[top, pl.ds(cols, cols)] = imag
        xs[low, pl.ds(0, cols)] = -imag
        xs[low, pl.ds(cols, cols)] = real

    for copy in loads:
        copy.wait()
    base[...] = mm(leaf2[...], xs[...])
    rounded = base[...].astype(BF16)
    xb[pl.ds(0, interior), :] = rounded
    xb[pl.ds(interior, interior), pl.ds(0, cols)] = -rounded[:, cols:]
    xb[pl.ds(interior, interior), pl.ds(cols, cols)] = rounded[:, :cols]
    resid0[...] = mm(cpl2[...], xb[...])

    has_next = jnp.where(s < last, fronts, 0)
    has_prev = jnp.where(s > 0, 1, 0)
    pl.semaphore_wait(barrier, fronts - 1 + has_next + has_prev)

    def send_tag(i, carry):
        pltpu.make_async_remote_copy(
            src_ref=tab_ref,
            dst_ref=tag_recv.at[f],
            send_sem=tag_send,
            recv_sem=tag_arrive,
            device_id=(s, peer(i)),
            device_id_type=MESH,
        ).start()
        return carry

    lax.fori_loop(0, fronts - 1, send_tag, 0)
    tag_recv[f] = tab_ref[...]

    def prev_copy(slab_to):
        return pltpu.make_async_remote_copy(
            src_ref=tab_ref,
            dst_ref=tab_recv,
            send_sem=prev_send,
            recv_sem=prev_arrive,
            device_id=(slab_to, f),
            device_id_type=MESH,
        )

    def home_copy(slab_to):
        return pltpu.make_async_remote_copy(
            src_ref=inc,
            dst_ref=home,
            send_sem=home_send,
            recv_sem=home_arrive,
            device_id=(slab_to, f),
            device_id_type=MESH,
        )

    @pl.when(s < last)
    def _():
        prev_copy(s + 1).start()

    def await_bytes(buf, count, sem):
        view = buf.at[pl.ds(0, count)]
        pltpu.make_async_copy(view, view, sem).wait()

    def send_blocks(source, target, send_sem, recv_sem, slab_to, count):
        def one(i, carry):
            to = peer(i)
            pltpu.make_async_remote_copy(
                src_ref=source.at[pl.ds(2 * to, 2)],
                dst_ref=target.at[pl.ds(2 * f, 2)],
                send_sem=send_sem,
                recv_sem=recv_sem,
                device_id=(slab_to, to),
                device_id_type=MESH,
            ).start()
            return carry

        lax.fori_loop(0, count, one, 0)

    @pl.when(s == 0)
    def _():
        resid = resid0[...].astype(BF16)
        rblk[pl.ds(0, pieces), 0] = resid[:, :cols].reshape(pieces, rows, cols)
        rblk[pl.ds(0, pieces), 1] = resid[:, cols:].reshape(pieces, rows, cols)

    @pl.when(s > 0)
    def _():
        near = leaf2[:, pl.ds(0, 2 * bnd)]
        left = mm(cpl2[:, pl.ds(0, interior)], near)
        right = mm(cpl2[:, pl.ds(interior, interior)], near)
        comp2[:, pl.ds(0, bnd)] = (left[:, :bnd] - right[:, bnd:]).astype(BF16)
        comp2[:, pl.ds(bnd, bnd)] = (left[:, bnd:] + right[:, :bnd]).astype(BF16)
        prev_copy(s).wait_recv()
        bring = pltpu.make_async_copy(tab_recv, prev_smem, smem_sem)
        bring.start()
        bring.wait()
        await_bytes(recv_b, cap, b_arrive)
        for p in range(pieces):
            block = recv_b[prev_smem[2, p]]
            inc[p] = block
            at, low = pl.ds(p * rows, rows), pl.ds(bnd + p * rows, rows)
            xin[at, pl.ds(0, cols)] = block[0]
            xin[at, pl.ds(cols, cols)] = block[1]
            xin[low, pl.ds(0, cols)] = -block[1]
            xin[low, pl.ds(cols, cols)] = block[0]
        resid = (resid0[...] + mm(comp2[...], xin[...])).astype(BF16)
        rblk[pl.ds(0, pieces), 0] = resid[:, :cols].reshape(pieces, rows, cols)
        rblk[pl.ds(0, pieces), 1] = resid[:, cols:].reshape(pieces, rows, cols)

    for i in range(cap):
        out_a[i] = rblk[tab_smem[0, i]]
    send_blocks(out_a, recv_a, a_send, a_arrive, s, fronts - 1)
    for k in range(2):
        recv_a[2 * f + k] = out_a[2 * f + k]

    @pl.when(s > 0)
    def _():
        home_copy(s - 1).start()
        full = base[...] + mm(leaf2[:, pl.ds(0, 2 * bnd)], xin[...])
        sol_ref[0] = full[:, :cols].astype(BF16)
        sol_ref[1] = full[:, cols:].astype(BF16)

    @pl.when(s == 0)
    def _():
        sol_ref[0] = base[:, pl.ds(0, cols)].astype(BF16)
        sol_ref[1] = base[:, pl.ds(cols, cols)].astype(BF16)

    await_bytes(tag_recv, fronts - 1, tag_arrive)
    tags = tag_recv[:, 1, :]
    lane = lax.broadcasted_iota(jnp.int32, (fronts, LANES), 1)
    row = lax.broadcasted_iota(jnp.int32, (fronts, LANES), 0)
    first = jnp.sum(jnp.where(lane == 2 * f, tags, 0), axis=1, keepdims=True)
    second = jnp.sum(jnp.where(lane == 2 * f + 1, tags, 0), axis=1, keepdims=True)
    picked = jnp.where(lane % 2 == 0, first, second)
    back = jnp.sum(jnp.where(row == lane // 2, picked, 0), axis=0, keepdims=True)
    col = jnp.concatenate([first, second], axis=0)
    wide_lane = lax.broadcasted_iota(jnp.int32, (cap, LANES), 1)
    wide_row = lax.broadcasted_iota(jnp.int32, (cap, LANES), 0)
    as_row = jnp.sum(jnp.where(wide_lane == wide_row, col, 0), axis=0, keepdims=True)
    valid = wide_lane < cap
    same = valid & (as_row == col) & (wide_lane < wide_row)
    below = valid & (as_row < col)
    rank = jnp.sum(jnp.where(same | below, 1, 0), axis=1, keepdims=True)
    repeat = jnp.max(jnp.where(same, 1, 0), axis=1, keepdims=True)
    placed = rank == wide_lane
    where_at = wide_row % fronts * 2 + wide_row // fronts
    order = jnp.sum(jnp.where(placed, where_at, 0), axis=0, keepdims=True)
    keep = jnp.sum(jnp.where(placed, repeat, 0), axis=0, keepdims=True)
    upto = jnp.sum(jnp.where(col <= wide_lane, 1, 0), axis=0, keepdims=True)
    hit = jnp.max(jnp.where(col == wide_lane, 1, 0), axis=0, keepdims=True)
    ends = jnp.where(hit > 0, upto - 1, cap)
    own_tab[0:1, :] = order
    own_tab[1:2, :] = keep
    own_tab[2:3, :] = ends
    own_tab[3:4, :] = back
    own_tab[4:8, :] = jnp.zeros((4, LANES), jnp.int32)
    bring = pltpu.make_async_copy(own_tab, own_smem, smem_sem)
    bring.start()
    bring.wait()
    for copy in sep_loads:
        copy.wait()

    await_bytes(recv_a, cap - 2, a_arrive)
    total = jnp.zeros((2, rows, cols), F32)
    for i in range(cap):
        block = recv_a[own_smem[0, i]].astype(F32)
        total = jnp.where(own_smem[1, i] > 0, total, 0.0) + block
        run[i] = total
    for m in range(slots):
        for q in range(parts):
            block = run[own_smem[2, m * parts + q]].astype(BF16)
            at, low = pl.ds(q * rows, rows), pl.ds(sepw + q * rows, rows)
            xsep[m, at, pl.ds(0, cols)] = block[0]
            xsep[m, at, pl.ds(cols, cols)] = block[1]
            xsep[m, low, pl.ds(0, cols)] = -block[1]
            xsep[m, low, pl.ds(cols, cols)] = block[0]
    for m in range(slots):
        value = mm(sep2[m], xsep[m]).astype(BF16)
        at = pl.ds(m * parts, parts)
        vals[at, 0] = value[:, :cols].reshape(parts, rows, cols)
        vals[at, 1] = value[:, cols:].reshape(parts, rows, cols)
    for i in range(cap):
        out_b[i] = vals[own_smem[3, i]]

    @pl.when(s < last)
    def _():
        send_blocks(out_b, recv_b, b_send, b_arrive, s + 1, fronts)
        home_copy(s).wait_recv()
        trace_ref[...] = home[...]
        await_bytes(out_b, cap, b_send)
        prev_copy(s).wait_send()

    @pl.when(s == last)
    def _():
        send_blocks(out_b, recv_t, b_send, t_arrive, s, fronts - 1)
        for k in range(2):
            recv_t[2 * f + k] = out_b[2 * f + k]
        await_bytes(recv_t, cap - 2, t_arrive)
        for p in range(pieces):
            trace_ref[p] = recv_t[tab_smem[2, p]]
        await_bytes(out_b, cap - 2, b_send)

    @pl.when(s > 0)
    def _():
        home_copy(s).wait_send()

    await_bytes(out_a, cap - 2, a_send)
    await_bytes(tag_recv, fronts - 1, tag_send)


def tables(owners, count, targets, part_count, pieces, positions, fronts):
    sep_ids = jnp.arange(owners.shape[0], dtype=jnp.int32)
    earlier = (owners[:, None] == owners[None, :]) & (sep_ids[:, None] > sep_ids[None, :])
    slot_of = jnp.sum(jnp.where(earlier, 1, 0), axis=1).astype(jnp.int32)
    sep_of = targets // part_count
    match = sep_of[:, None] == sep_ids[None, :]
    destination = jnp.sum(jnp.where(match, owners[None, :], 0), axis=1)
    slot = jnp.sum(jnp.where(match, slot_of[None, :], 0), axis=1)
    position = slot * part_count + targets % part_count
    ids = jnp.arange(pieces, dtype=jnp.int32)
    usable = ids < count
    before = (
        (destination[:, None] == destination[None, :])
        & usable[None, :]
        & (ids[None, :] < ids[:, None])
    )
    rank = jnp.sum(jnp.where(before, 1, 0), axis=1).astype(jnp.int32)
    index = destination * 2 + rank
    lanes = jnp.arange(LANES, dtype=jnp.int32)
    route = (lanes[:, None] == index[None, :]) & usable[None, :]
    out_src = jnp.sum(jnp.where(route, ids[None, :] - pieces, 0), axis=1) + pieces
    tag = jnp.sum(jnp.where(route, position[None, :] - positions, 0), axis=1) + positions
    back = jnp.where(usable, index, 2 * fronts)
    back = jnp.pad(back, (0, LANES - pieces))
    blank = jnp.zeros((LANES,), jnp.int32)
    return jnp.stack([out_src, tag, back, blank, blank, blank, blank, blank]).astype(jnp.int32)


def solution(mesh):
    slabs, fronts = mesh.shape["slab"], mesh.shape["front"]
    ring = 4

    def body(source, leaf_inverse, boundary_map, sep_inverse, owner_map, piece_count, piece_target):
        src = source[0, 0]
        inv = leaf_inverse[0, 0]
        cpl = boundary_map[0, 0]
        sep = sep_inverse[0]
        interior, cols = src.shape[1], src.shape[2]
        bnd = cpl.shape[1]
        pieces = piece_target.shape[2]
        rows = bnd // pieces
        slots, sepw = sep.shape[0], sep.shape[2]
        parts = sepw // rows
        positions = slots * parts
        cap = 2 * fronts
        halves = interior // bnd
        tab = tables(
            owner_map[0], piece_count[0, 0], piece_target[0, 0], parts, pieces, positions, fronts
        )

        def blocks(count, dtype=BF16):
            return pltpu.VMEM((count, 2, rows, cols), dtype)

        vmem = pl.BlockSpec(memory_space=pltpu.VMEM)
        anyspace = pl.BlockSpec(memory_space=pl.ANY)
        smem = pl.BlockSpec(memory_space=pltpu.SMEM)
        dma = pltpu.SemaphoreType.DMA
        solved, trace = pl.pallas_call(
            functools.partial(sweep_kernel, slabs, fronts, ring),
            out_shape=(
                jax.ShapeDtypeStruct((2, interior, cols), BF16),
                jax.ShapeDtypeStruct((pieces, 2, rows, cols), BF16),
            ),
            in_specs=[vmem, anyspace, anyspace, anyspace, vmem, smem],
            out_specs=(vmem, vmem),
            scratch_shapes=[
                pltpu.VMEM((interior, 2 * interior), BF16),
                pltpu.VMEM((bnd, 2 * interior), BF16),
                pltpu.VMEM((slots, sepw, 2 * sepw), BF16),
                pltpu.VMEM((bnd, 2 * bnd), BF16),
                pltpu.VMEM((2 * interior, 2 * cols), BF16),
                pltpu.VMEM((2 * interior, 2 * cols), BF16),
                pltpu.VMEM((2 * bnd, 2 * cols), BF16),
                pltpu.VMEM((slots, 2 * sepw, 2 * cols), BF16),
                pltpu.VMEM((interior, 2 * cols), F32),
                pltpu.VMEM((bnd, 2 * cols), F32),
                blocks(pieces + 1),
                blocks(pieces),
                blocks(cap),
                blocks(cap),
                blocks(cap + 1, F32),
                blocks(positions + 1),
                blocks(cap),
                blocks(cap + 1),
                blocks(cap + 1),
                blocks(pieces),
                pltpu.VMEM((fronts, 8, LANES), jnp.int32),
                pltpu.VMEM((8, LANES), jnp.int32),
                pltpu.VMEM((8, LANES), jnp.int32),
                pltpu.SMEM((8, LANES), jnp.int32),
                pltpu.SMEM((8, LANES), jnp.int32),
                dma((2 * halves + 2,)),
                dma((2 * slots,)),
                dma,
                dma,
                dma,
                dma,
                dma,
                dma,
                dma,
                dma,
                dma,
                dma,
                dma,
                dma,
            ],
            compiler_params=pltpu.CompilerParams(
                collective_id=0, has_side_effects=True, vmem_limit_bytes=48 * 1024 * 1024
            ),
        )(src, inv, cpl, sep, tab, tab)
        return solved[None, None], trace[None, None]

    return jax.shard_map(
        body,
        mesh=mesh,
        in_specs=(
            P("slab", "front", None, None, None),
            P("slab", "front", None, None, None),
            P("slab", "front", None, None, None),
            P("slab", "front", None, None, None),
            P("slab", None),
            P("slab", "front"),
            P("slab", "front", None),
        ),
        out_specs=(
            P("slab", "front", None, None, None),
            P("slab", "front", None, None, None, None),
        ),
        check_vma=False,
    )
```

time: 566 us -> 184 us (0.33)
  the two profiles are of different devices: /device:TPU:8 before, /device:TPU:25 now
where the time goes in v1:
time: 184 us
  Pallas kernels  174 us (95%)
  local copies, waits for them, and re-layouts  5.19 us (3%)
  other arithmetic  3.39 us (2%)
    pallas_call x1, Pallas kernels, body(): pl.pallas_call(functools.partial(sweep_kernel, slabs, fronts, ring), out_...  174 us
    unnamed x8, local copies, waits for them, and re-layouts  5.16 us

profile of v1, /device:TPU:25, one launch (start us, length us, event | category | flops | bytes accessed | tf_op | source)
XLA Modules:
  0.0 184.1 jit_solution(8960742914920713629)
XLA Ops:
  1.3 0.9 select_reduce_fusion
  2.2 0.7 fusion.3
  2.9 0.8 select_reduce_fusion.2
  3.7 0.2 select_reduce_fusion.4
  3.9 0.7 broadcast_select_fusion
  4.6 0.1 select_reduce_fusion.1
  4.8 0.0 copy-start
  4.8 1.5 copy-done
  6.2 0.0 copy-start.1
  6.2 1.3 copy-done.1
  7.5 0.0 copy-start.2
  7.5 1.0 copy-done.2
  8.5 174.1 %shard_map.86 = (bf16[2,768,128]{2,1,0:T(8,128)(2,1)S(1)}, bf16[24,2,16,128]{3,2,1,0:T(8,128)(2,1)S(1)}) custom-call(bf16[2,768,128]{2,1,0:T(8,128)(2,1)S(1)} %bitcast.29, bf16[2,768,768]{2,1,0:T(8,128)(2,1)} %bitcast.32, bf16[2,384,768]{2,1,0:T(8,128)(2,1)S(1)} %bitcast.28, bf16[3,2,384,384]{3,2,1,0:T(8,128)(2,1)S(1)} %bitcast.27, ...), custom_call_target="tpu_custom_call" | custom-call | tf_op jit(solution)/shard_map/pallas_call | solution.py:419
  182.6 0.7 copy.12
  183.4 0.7 copy.13
  (8 shorter events, 0.0 us)
Async XLA Ops:
  4.8 1.5 copy-start
  6.2 1.3 copy-start.1
  7.5 1.0 copy-start.2

commit v2 on v1

v2 whole, which is shorter than its diff:
```python
import functools

import jax
import jax.numpy as jnp
from jax import lax
from jax.experimental import pallas as pl
from jax.experimental.pallas import tpu as pltpu
from jax.sharding import PartitionSpec as P

MESH = pl.DeviceIdType.MESH
BF16 = jnp.bfloat16
F32 = jnp.float32
I32 = jnp.int32
LANES = 128
HALF = LANES // 2
BATCHES = 2


def mm(a, b):
    return jnp.dot(a, b, preferred_element_type=F32)


def turn(x):
    return pltpu.roll(x, HALF, 1)


def iota(shape, axis):
    return lax.broadcasted_iota(I32, shape, axis)


def total(mask, value, axis):
    return jnp.sum(jnp.where(mask, value, 0), axis=axis, keepdims=True)


def as_column(row_value, size):
    shape = (size, size)
    return total(iota(shape, 0) == iota(shape, 1), row_value, 1)


def as_row(column, size):
    shape = (size, LANES)
    return total(iota(shape, 0) == iota(shape, 1), column, 0)


def leaf_tables(owners, targets, count, parts, positions, fronts):
    seps, pieces = owners.shape[1], targets.shape[1]
    square = (seps, seps)
    owner_col = as_column(owners, seps)
    slot_row = total((owner_col == owners) & (iota(square, 0) < iota(square, 1)), 1, 0)
    target_col = as_column(targets, pieces)
    wide = (pieces, seps)
    sep_id = iota(wide, 1)
    match = (target_col >= sep_id * parts) & (target_col < sep_id * parts + parts)
    destination = total(match, owners, 1)
    position = total(match, (slot_row - sep_id) * parts, 1) + target_col
    small = (pieces, pieces)
    piece_col, piece_row = iota(small, 0), iota(small, 1)
    destination_row = total(piece_col == piece_row, destination, 0)
    before = (destination == destination_row) & (piece_row < count) & (piece_row < piece_col)
    index = destination * 2 + total(before, 1, 1)
    shape = (pieces, LANES)
    piece_id, lane = iota(shape, 0), iota(shape, 1)
    usable = piece_id < count
    route = (lane == index) & usable
    out_src = total(route, piece_id - pieces, 0) + pieces
    tag = total(route, position - positions, 0) + positions
    back = total(piece_id == lane, jnp.where(usable, index, 2 * fronts), 0)
    return out_src, tag, back


def owner_tables(tags, f, fronts):
    cap = 2 * fronts
    lane, row = iota((fronts, LANES), 1), iota((fronts, LANES), 0)
    first = total(lane == 2 * f, tags, 1)
    second = total(lane == 2 * f + 1, tags, 1)
    picked = jnp.where(lane % 2 == 0, first, second)
    back = total(row == lane // 2, picked, 0)
    col = jnp.concatenate([first, second], axis=0)
    lane, row = iota((cap, LANES), 1), iota((cap, LANES), 0)
    tag_row = as_row(col, cap)
    valid = lane < cap
    same = valid & (tag_row == col) & (lane < row)
    rank = total(same | (valid & (tag_row < col)), 1, 1)
    repeat = jnp.max(jnp.where(same, 1, 0), axis=1, keepdims=True)
    placed = rank == lane
    order = total(placed, row % fronts * 2 + row // fronts, 0)
    keep = total(placed, repeat, 0)
    upto = total(col <= lane, 1, 0)
    hit = total(col == lane, 1, 0)
    ends = jnp.where(hit > 0, upto - 1, cap)
    return order, keep, ends, back


def sweep_kernel(
    slabs,
    fronts,
    ring,
    src_hbm,
    inv_hbm,
    cpl_hbm,
    sep_hbm,
    own_hbm,
    cnt_hbm,
    tgt_hbm,
    sol_ref,
    trace_ref,
    src_v,
    own_v,
    tgt_v,
    cnt_s,
    leaf2,
    cpl2,
    sep2,
    comp2,
    xs,
    xb,
    xin,
    xsep,
    base,
    resid0,
    rblk,
    inc,
    out_a,
    recv_a0,
    recv_a1,
    run,
    vals,
    out_b,
    recv_b0,
    recv_b1,
    recv_t,
    home,
    tag_v,
    tag_recv,
    leaf_tab,
    prev_tab,
    own_tab,
    leaf_smem,
    prev_smem,
    own_smem,
    small_sem,
    load_sem,
    sep_sem,
    tag_send,
    tag_arrive,
    prev_send,
    prev_arrive,
    a_send,
    a_arrive,
    b_send,
    b_arrive,
    t_arrive,
    home_send,
    home_arrive,
    smem_sem,
):
    s = lax.axis_index("slab")
    f = lax.axis_index("front")
    last = slabs - 1
    interior = src_v.shape[1]
    bnd = cpl2.shape[0]
    slots, sepw = sep2.shape[0], sep2.shape[1]
    pieces = inc.shape[0]
    rows = inc.shape[2]
    parts = sepw // rows
    positions = slots * parts
    cap = 2 * fronts
    halves = interior // bnd
    depth = fronts // ring
    recv_a, recv_b = (recv_a0, recv_a1), (recv_b0, recv_b1)
    lane_sets = [pl.ds(b * LANES, LANES) for b in range(BATCHES)]

    def peer(i):
        j, k = i // ring, i % ring
        dz = depth // 2 + (1 - 2 * (j % 2)) * ((j + 1) // 2)
        dx = ring // 2 + (1 - 2 * (k % 2)) * ((k + 1) // 2)
        return (f // ring + dz) % depth * ring + (f % ring + dx) % ring

    barrier = pltpu.get_barrier_semaphore()

    def greet(slab_to, count):
        def one(i, carry):
            pl.semaphore_signal(
                barrier, inc=1, device_id=(slab_to, peer(i)), device_id_type=MESH
            )
            return carry

        lax.fori_loop(0, count, one, 0)

    smalls = [
        pltpu.make_async_copy(own_hbm, own_v, small_sem.at[0]),
        pltpu.make_async_copy(tgt_hbm, tgt_v, small_sem.at[1]),
        pltpu.make_async_copy(cnt_hbm, cnt_s, small_sem.at[2]),
    ]
    load_src = pltpu.make_async_copy(src_hbm, src_v, small_sem.at[3])
    loads = []
    for h in range(halves):
        for c in range(2):
            at = (2 * h + c) * bnd
            loads.append(
                pltpu.make_async_copy(
                    inv_hbm.at[c, :, pl.ds(h * bnd, bnd)],
                    leaf2.at[:, pl.ds(at, bnd)],
                    load_sem.at[2 * h + c],
                )
            )
    cpl_loads = []
    for c in range(2):
        cpl_loads.append(
            pltpu.make_async_copy(
                cpl_hbm.at[c],
                cpl2.at[:, pl.ds(c * interior, interior)],
                load_sem.at[2 * halves + c],
            )
        )
    sep_loads = []
    for m in range(slots):
        for c in range(2):
            sep_loads.append(
                pltpu.make_async_copy(
                    sep_hbm.at[m, c],
                    sep2.at[m, :, pl.ds(c * sepw, sepw)],
                    sep_sem.at[2 * m + c],
                )
            )
    for copy in smalls + [load_src] + loads + cpl_loads:
        copy.start()

    @pl.when(s > 0)
    def _():
        greet(s - 1, fronts)

    greet(s, fronts - 1)

    @pl.when(s < last)
    def _():
        pl.semaphore_signal(barrier, inc=1, device_id=(s + 1, f), device_id_type=MESH)

    for copy in sep_loads:
        copy.start()

    zero_block = jnp.zeros((rows, LANES), BF16)
    run[cap] = jnp.zeros((rows, LANES), F32)
    for b in range(BATCHES):
        rblk[b, pieces] = zero_block
        vals[b, positions] = zero_block
        recv_b[b][cap] = zero_block
        recv_t[b, cap] = zero_block

    for copy in smalls:
        copy.wait()
    out_src, tag, back = leaf_tables(
        own_v[...], tgt_v[...], cnt_s[0, 0], parts, positions, fronts
    )
    leaf_tab[0:1, :] = out_src
    leaf_tab[1:2, :] = back
    leaf_tab[2:8, :] = jnp.zeros((6, LANES), I32)
    tag_v[...] = tag
    bring = pltpu.make_async_copy(leaf_tab, leaf_smem, smem_sem.at[0])
    bring.start()

    def low_half(like):
        return iota(like.shape, 1) < HALF

    def swap(x):
        turned = turn(x)
        return jnp.where(low_half(x), -turned, turned)

    load_src.wait()
    for h in range(halves):
        real = src_v[0, pl.ds(h * bnd, bnd), :]
        imag = src_v[1, pl.ds(h * bnd, bnd), :]
        top, low = pl.ds(2 * h * bnd, bnd), pl.ds((2 * h + 1) * bnd, bnd)
        packed = (
            jnp.where(low_half(real), real, turn(imag)),
            jnp.where(low_half(real), turn(real), imag),
        )
        for b in range(BATCHES):
            xs[top, lane_sets[b]] = packed[b]
            xs[low, lane_sets[b]] = swap(packed[b])

    for copy in loads:
        copy.wait()
    base[...] = mm(leaf2[...], xs[...])
    for b in range(BATCHES):
        rounded = base[:, lane_sets[b]].astype(BF16)
        xb[pl.ds(0, interior), lane_sets[b]] = rounded
        xb[pl.ds(interior, interior), lane_sets[b]] = swap(rounded)
    for copy in cpl_loads:
        copy.wait()
    resid0[...] = mm(cpl2[...], xb[...])
    bring.wait()

    has_next = jnp.where(s < last, fronts, 0)
    has_prev = jnp.where(s > 0, 1, 0)
    pl.semaphore_wait(barrier, fronts - 1 + has_next + has_prev)

    def push_tag(to):
        pltpu.make_async_remote_copy(
            src_ref=tag_v,
            dst_ref=tag_recv.at[f],
            send_sem=tag_send,
            recv_sem=tag_arrive,
            device_id=(s, to),
            device_id_type=MESH,
        ).start()

    def send_blocks(source, target, send_sem, recv_sem, slab_to, count, tagged=False):
        def one(i, carry):
            to = peer(i)
            if tagged:
                push_tag(to)
            pltpu.make_async_remote_copy(
                src_ref=source.at[pl.ds(2 * to, 2)],
                dst_ref=target.at[pl.ds(2 * f, 2)],
                send_sem=send_sem,
                recv_sem=recv_sem,
                device_id=(slab_to, to),
                device_id_type=MESH,
            ).start()
            return carry

        lax.fori_loop(0, count, one, 0)

    def prev_copy(slab_to):
        return pltpu.make_async_remote_copy(
            src_ref=leaf_tab,
            dst_ref=prev_tab,
            send_sem=prev_send,
            recv_sem=prev_arrive,
            device_id=(slab_to, f),
            device_id_type=MESH,
        )

    def home_copy(slab_to):
        return pltpu.make_async_remote_copy(
            src_ref=inc,
            dst_ref=home,
            send_sem=home_send,
            recv_sem=home_arrive,
            device_id=(slab_to, f),
            device_id_type=MESH,
        )

    def await_bytes(buf, count, sem):
        view = buf.at[pl.ds(0, count)]
        pltpu.make_async_copy(view, view, sem).wait()

    def push_resid(b, resid, tagged):
        rblk[b, pl.ds(0, pieces)] = resid.astype(BF16).reshape(pieces, rows, LANES)
        for i in range(cap):
            out_a[b, i] = rblk[b, leaf_smem[0, i]]
        send_blocks(
            out_a.at[b], recv_a[b], a_send.at[b], a_arrive.at[b], s, fronts - 1, tagged
        )
        for k in range(2):
            recv_a[b][2 * f + k] = out_a[b, 2 * f + k]

    def make_owner_tables():
        await_bytes(tag_recv, fronts - 1, tag_arrive)
        order, keep, ends, ret = owner_tables(tag_recv[:, 0, :], f, fronts)
        own_tab[0:1, :] = order
        own_tab[1:2, :] = keep
        own_tab[2:3, :] = ends
        own_tab[3:4, :] = ret
        own_tab[4:8, :] = jnp.zeros((4, LANES), I32)
        bring = pltpu.make_async_copy(own_tab, own_smem, smem_sem.at[1])
        bring.start()
        bring.wait()

    def unpack(b0, b1):
        first = low_half(b0)
        return jnp.where(first, b0, turn(b1)), jnp.where(first, turn(b0), b1)

    tag_recv[f] = tag_v[...]

    @pl.when(s == 0)
    def _():
        for b in range(BATCHES):
            push_resid(b, resid0[:, lane_sets[b]], b == 0)
        prev_copy(s + 1).start()
        real, imag = unpack(base[:, lane_sets[0]], base[:, lane_sets[1]])
        sol_ref[0] = real.astype(BF16)
        sol_ref[1] = imag.astype(BF16)
        make_owner_tables()

    @pl.when(s > 0)
    def _():
        def one(i, carry):
            push_tag(peer(i))
            return carry

        lax.fori_loop(0, fronts - 1, one, 0)

        @pl.when(s < last)
        def _():
            prev_copy(s + 1).start()

        near = leaf2[:, pl.ds(0, 2 * bnd)]
        left = mm(cpl2[:, pl.ds(0, interior)], near)
        right = mm(cpl2[:, pl.ds(interior, interior)], near)
        comp2[:, pl.ds(0, bnd)] = (left[:, :bnd] - right[:, bnd:]).astype(BF16)
        comp2[:, pl.ds(bnd, bnd)] = (left[:, bnd:] + right[:, :bnd]).astype(BF16)
        prev_copy(s).wait_recv()
        bring = pltpu.make_async_copy(prev_tab, prev_smem, smem_sem.at[0])
        bring.start()
        bring.wait()
        make_owner_tables()
        for b in range(BATCHES):
            await_bytes(recv_b[b], cap, b_arrive.at[b])
            for p in range(pieces):
                block = recv_b[b][prev_smem[1, p]]
                xin[pl.ds(p * rows, rows), lane_sets[b]] = block
                xin[pl.ds(bnd + p * rows, rows), lane_sets[b]] = swap(block)
            push_resid(b, resid0[:, lane_sets[b]] + mm(comp2[...], xin[:, lane_sets[b]]), False)
        for p in range(pieces):
            at = pl.ds(p * rows, rows)
            real, imag = unpack(xin[at, lane_sets[0]], xin[at, lane_sets[1]])
            inc[p, 0] = real
            inc[p, 1] = imag
        home_copy(s - 1).start()
        full = base[...] + mm(leaf2[:, pl.ds(0, 2 * bnd)], xin[...])
        real, imag = unpack(full[:, :LANES], full[:, LANES:])
        sol_ref[0] = real.astype(BF16)
        sol_ref[1] = imag.astype(BF16)

    for copy in sep_loads:
        copy.wait()

    for b in range(BATCHES):
        await_bytes(recv_a[b], cap - 2, a_arrive.at[b])
        running = jnp.zeros((rows, LANES), F32)
        for i in range(cap):
            block = recv_a[b][own_smem[0, i]].astype(F32)
            running = jnp.where(own_smem[1, i] > 0, running, 0.0) + block
            run[i] = running
        for m in range(slots):
            for q in range(parts):
                block = run[own_smem[2, m * parts + q]].astype(BF16)
                xsep[m, pl.ds(q * rows, rows), :] = block
                xsep[m, pl.ds(sepw + q * rows, rows), :] = swap(block)
        for m in range(slots):
            value = mm(sep2[m], xsep[m]).astype(BF16)
            vals[b, pl.ds(m * parts, parts)] = value.reshape(parts, rows, LANES)
        for i in range(cap):
            out_b[b, i] = vals[b, own_smem[3, i]]

        @pl.when(s < last)
        def _():
            send_blocks(
                out_b.at[b], recv_b[b], b_send.at[b], b_arrive.at[b], s + 1, fronts
            )

        @pl.when(s == last)
        def _():
            send_blocks(
                out_b.at[b], recv_t.at[b], b_send.at[b], t_arrive.at[b], s, fronts - 1
            )
            for k in range(2):
                recv_t[b, 2 * f + k] = out_b[b, 2 * f + k]

    @pl.when(s < last)
    def _():
        home_copy(s).wait_recv()
        trace_ref[...] = home[...]
        for b in range(BATCHES):
            await_bytes(out_b.at[b], cap, b_send.at[b])
        prev_copy(s).wait_send()

    @pl.when(s == last)
    def _():
        for b in range(BATCHES):
            await_bytes(recv_t.at[b], cap - 2, t_arrive.at[b])
        for p in range(pieces):
            at = leaf_smem[1, p]
            real, imag = unpack(recv_t[0, at], recv_t[1, at])
            trace_ref[p, 0] = real
            trace_ref[p, 1] = imag
        for b in range(BATCHES):
            await_bytes(out_b.at[b], cap - 2, b_send.at[b])

    @pl.when(s > 0)
    def _():
        home_copy(s).wait_send()

    for b in range(BATCHES):
        await_bytes(out_a.at[b], cap - 2, a_send.at[b])
    await_bytes(tag_recv, fronts - 1, tag_send)


def solution(mesh):
    slabs, fronts = mesh.shape["slab"], mesh.shape["front"]
    ring = 4

    def body(source, leaf_inverse, boundary_map, sep_inverse, owner_map, piece_count, piece_target):
        src = source[0, 0]
        inv = leaf_inverse[0, 0]
        cpl = boundary_map[0, 0]
        sep = sep_inverse[0]
        interior, cols = src.shape[1], src.shape[2]
        bnd = cpl.shape[1]
        seps, pieces = owner_map.shape[1], piece_target.shape[2]
        rows = bnd // pieces
        slots, sepw = sep.shape[0], sep.shape[2]
        positions = slots * (sepw // rows)
        cap = 2 * fronts
        halves = interior // bnd

        def blocks(count):
            return pltpu.VMEM((BATCHES, count, rows, LANES), BF16)

        def single(count):
            return pltpu.VMEM((count, rows, LANES), BF16)

        vmem = pl.BlockSpec(memory_space=pltpu.VMEM)
        anyspace = pl.BlockSpec(memory_space=pl.ANY)
        dma = pltpu.SemaphoreType.DMA
        table = pltpu.VMEM((8, LANES), I32)
        smem_table = pltpu.SMEM((8, LANES), I32)
        solved, trace = pl.pallas_call(
            functools.partial(sweep_kernel, slabs, fronts, ring),
            out_shape=(
                jax.ShapeDtypeStruct((2, interior, cols), BF16),
                jax.ShapeDtypeStruct((pieces, 2, rows, cols), BF16),
            ),
            in_specs=[anyspace] * 7,
            out_specs=(vmem, vmem),
            scratch_shapes=[
                pltpu.VMEM((2, interior, cols), BF16),
                pltpu.VMEM((1, seps), I32),
                pltpu.VMEM((1, pieces), I32),
                pltpu.SMEM((1, 1), I32),
                pltpu.VMEM((interior, 2 * interior), BF16),
                pltpu.VMEM((bnd, 2 * interior), BF16),
                pltpu.VMEM((slots, sepw, 2 * sepw), BF16),
                pltpu.VMEM((bnd, 2 * bnd), BF16),
                pltpu.VMEM((2 * interior, 2 * cols), BF16),
                pltpu.VMEM((2 * interior, 2 * cols), BF16),
                pltpu.VMEM((2 * bnd, 2 * cols), BF16),
                pltpu.VMEM((slots, 2 * sepw, LANES), BF16),
                pltpu.VMEM((interior, 2 * cols), F32),
                pltpu.VMEM((bnd, 2 * cols), F32),
                blocks(pieces + 1),
                pltpu.VMEM((pieces, 2, rows, cols), BF16),
                blocks(cap),
                single(cap),
                single(cap),
                pltpu.VMEM((cap + 1, rows, LANES), F32),
                blocks(positions + 1),
                blocks(cap),
                single(cap + 1),
                single(cap + 1),
                blocks(cap + 1),
                pltpu.VMEM((pieces, 2, rows, cols), BF16),
                pltpu.VMEM((1, LANES), I32),
                pltpu.VMEM((fronts, 1, LANES), I32),
                table,
                table,
                table,
                smem_table,
                smem_table,
                smem_table,
                dma((4,)),
                dma((2 * halves + 2,)),
                dma((2 * slots,)),
                dma,
                dma,
                dma,
                dma,
                dma((BATCHES,)),
                dma((BATCHES,)),
                dma((BATCHES,)),
                dma((BATCHES,)),
                dma((BATCHES,)),
                dma,
                dma,
                dma((2,)),
            ],
            compiler_params=pltpu.CompilerParams(
                collective_id=0, has_side_effects=True, vmem_limit_bytes=60 * 1024 * 1024
            ),
        )(src, inv, cpl, sep, owner_map, piece_count, piece_target[0])
        return solved[None, None], trace[None, None]

    return jax.shard_map(
        body,
        mesh=mesh,
        in_specs=(
            P("slab", "front", None, None, None),
            P("slab", "front", None, None, None),
            P("slab", "front", None, None, None),
            P("slab", "front", None, None, None),
            P("slab", None),
            P("slab", "front"),
            P("slab", "front", None),
        ),
        out_specs=(
            P("slab", "front", None, None, None),
            P("slab", "front", None, None, None, None),
        ),
        check_vma=False,
    )
```

time: 184 us -> 140 us (0.76)
  Pallas kernels: 174 us -> 135 us
  other arithmetic: 3.39 us -> 0 us
    pallas_call x1, Pallas kernels: 174 us -> 135 us  [body(): pl.pallas_call(functools.partial(sweep_kernel, slabs, fronts, ring), out_...]
    reduce_sum x4 -> x0, other arithmetic: 2.02 us -> none  [the longest x1 0.91 us: tables(): slot_of = jnp.sum(jnp.where(earlier, 1, 0), axis=1).astype(jnp.int32)]
    unnamed x8 -> x2, local copies, waits for them, and re-layouts: 5.16 us -> 3.38 us
where the time goes in v2:
time: 140 us
  Pallas kernels  135 us (96%)
  local copies, waits for them, and re-layouts  3.38 us (2%)
    pallas_call x1, Pallas kernels, body(): pl.pallas_call(functools.partial(sweep_kernel, slabs, fronts, ring), out_...  135 us
    unnamed x2, local copies, waits for them, and re-layouts  3.38 us

profile of v2, /device:TPU:25, one launch (start us, length us, event | category | flops | bytes accessed | tf_op | source)
XLA Modules:
  0.0 140.1 jit_solution(15303636502276719742)
XLA Ops:
  1.3 135.4 %shard_map.86 = (bf16[2,768,128]{2,1,0:T(8,128)(2,1)}, bf16[24,2,16,128]{3,2,1,0:T(8,128)(2,1)}) custom-call(bf16[2,768,128]{2,1,0:T(8,128)(2,1)} %bitcast.10, bf16[2,768,768]{2,1,0:T(8,128)(2,1)} %bitcast.7, bf16[2,384,768]{2,1,0:T(8,128)(2,1)} %bitcast.9, bf16[3,2,384,384]{3,2,1,0:T(8,128)(2,1)} %bitcast.8, s32[1,64]{1,0:T(1,128)} %own_hbm.1, ...), custom_call_target="tpu_custom_call" | custom-call | tf_op jit(solution)/shard_map/pallas_call | solution.py:520
  136.7 1.8 %copy.12 = bf16[1,1,2,768,128]{4,3,2,1,0:T(8,128)(2,1)} copy(bf16[1,1,2,768,128]{4,3,2,1,0:T(8,128)(2,1)} %bitcast.11) | data formatting | bytes 786432
  138.5 1.6 %copy.13 = bf16[1,1,24,2,16,128]{5,4,3,2,1,0:T(8,128)(2,1)} copy(bf16[1,1,24,2,16,128]{5,4,3,2,1,0:T(8,128)(2,1)} %bitcast.12) | data formatting | bytes 393216

commit v3 on v2

--- a/solution.py
+++ b/solution.py
@@ -89,6 +89,20 @@
     hit = total(col == lane, 1, 0)
     ends = jnp.where(hit > 0, upto - 1, cap)
     return order, keep, ends, back
+
+
+def stay(x):
+    return pltpu.with_memory_space_constraint(x, pltpu.HBM)
+
+
+def around(size):
+    half = size // 2
+    return [half + (1 - 2 * (j % 2)) * ((j + 1) // 2) for j in range(size)]
+
+
+def ordered_offsets(depth, ring):
+    offsets = [(dz, dx) for dx in around(ring) for dz in around(depth)]
+    return sorted(offsets, key=lambda o: -min(o[0], depth - o[0]) - min(o[1], ring - o[1]))
 
 
 def sweep_kernel(
@@ -170,22 +184,19 @@
     recv_a, recv_b = (recv_a0, recv_a1), (recv_b0, recv_b1)
     lane_sets = [pl.ds(b * LANES, LANES) for b in range(BATCHES)]
 
-    def peer(i):
-        j, k = i // ring, i % ring
-        dz = depth // 2 + (1 - 2 * (j % 2)) * ((j + 1) // 2)
-        dx = ring // 2 + (1 - 2 * (k % 2)) * ((k + 1) // 2)
-        return (f // ring + dz) % depth * ring + (f % ring + dx) % ring
+    f_z, f_x = lax.div(f, ring), lax.rem(f, ring)
+    z_of = [lax.rem(f_z + dz, depth) * ring for dz in range(depth)]
+    x_of = [lax.rem(f_x + dx, ring) for dx in range(ring)]
+
+    def peers(count):
+        for dz, dx in ordered_offsets(depth, ring)[:count]:
+            yield z_of[dz] + x_of[dx]
 
     barrier = pltpu.get_barrier_semaphore()
 
     def greet(slab_to, count):
-        def one(i, carry):
-            pl.semaphore_signal(
-                barrier, inc=1, device_id=(slab_to, peer(i)), device_id_type=MESH
-            )
-            return carry
-
-        lax.fori_loop(0, count, one, 0)
+        for to in peers(count):
+            pl.semaphore_signal(barrier, inc=1, device_id=(slab_to, to), device_id_type=MESH)
 
     smalls = [
         pltpu.make_async_copy(own_hbm, own_v, small_sem.at[0]),
@@ -295,21 +306,19 @@
     has_prev = jnp.where(s > 0, 1, 0)
     pl.semaphore_wait(barrier, fronts - 1 + has_next + has_prev)
 
-    def push_tag(to):
-        pltpu.make_async_remote_copy(
-            src_ref=tag_v,
-            dst_ref=tag_recv.at[f],
-            send_sem=tag_send,
-            recv_sem=tag_arrive,
-            device_id=(s, to),
-            device_id_type=MESH,
-        ).start()
-
-    def send_blocks(source, target, send_sem, recv_sem, slab_to, count, tagged=False):
-        def one(i, carry):
-            to = peer(i)
-            if tagged:
-                push_tag(to)
+    def push_tags():
+        for to in peers(fronts - 1):
+            pltpu.make_async_remote_copy(
+                src_ref=tag_v,
+                dst_ref=tag_recv.at[f],
+                send_sem=tag_send,
+                recv_sem=tag_arrive,
+                device_id=(s, to),
+                device_id_type=MESH,
+            ).start()
+
+    def send_blocks(source, target, send_sem, recv_sem, slab_to, count):
+        for to in peers(count):
             pltpu.make_async_remote_copy(
                 src_ref=source.at[pl.ds(2 * to, 2)],
                 dst_ref=target.at[pl.ds(2 * f, 2)],
@@ -318,9 +327,6 @@
                 device_id=(slab_to, to),
                 device_id_type=MESH,
             ).start()
-            return carry
-
-        lax.fori_loop(0, count, one, 0)
 
     def prev_copy(slab_to):
         return pltpu.make_async_remote_copy(
@@ -346,13 +352,13 @@
         view = buf.at[pl.ds(0, count)]
         pltpu.make_async_copy(view, view, sem).wait()
 
-    def push_resid(b, resid, tagged):
+    def put_resid(b, resid):
         rblk[b, pl.ds(0, pieces)] = resid.astype(BF16).reshape(pieces, rows, LANES)
+
+    def push_resid(b):
         for i in range(cap):
             out_a[b, i] = rblk[b, leaf_smem[0, i]]
-        send_blocks(
-            out_a.at[b], recv_a[b], a_send.at[b], a_arrive.at[b], s, fronts - 1, tagged
-        )
+        send_blocks(out_a.at[b], recv_a[b], a_send.at[b], a_arrive.at[b], s, fronts - 1)
         for k in range(2):
             recv_a[b][2 * f + k] = out_a[b, 2 * f + k]
 
@@ -374,23 +380,9 @@
 
     tag_recv[f] = tag_v[...]
 
-    @pl.when(s == 0)
-    def _():
-        for b in range(BATCHES):
-            push_resid(b, resid0[:, lane_sets[b]], b == 0)
-        prev_copy(s + 1).start()
-        real, imag = unpack(base[:, lane_sets[0]], base[:, lane_sets[1]])
-        sol_ref[0] = real.astype(BF16)
-        sol_ref[1] = imag.astype(BF16)
-        make_owner_tables()
-
     @pl.when(s > 0)
     def _():
-        def one(i, carry):
-            push_tag(peer(i))
-            return carry
-
-        lax.fori_loop(0, fronts - 1, one, 0)
+        push_tags()
 
         @pl.when(s < last)
         def _():
@@ -406,13 +398,39 @@
         bring.start()
         bring.wait()
         make_owner_tables()
-        for b in range(BATCHES):
+
+    for b in range(BATCHES):
+
+        @pl.when(s > 0)
+        def _():
             await_bytes(recv_b[b], cap, b_arrive.at[b])
             for p in range(pieces):
                 block = recv_b[b][prev_smem[1, p]]
                 xin[pl.ds(p * rows, rows), lane_sets[b]] = block
                 xin[pl.ds(bnd + p * rows, rows), lane_sets[b]] = swap(block)
-            push_resid(b, resid0[:, lane_sets[b]] + mm(comp2[...], xin[:, lane_sets[b]]), False)
+            put_resid(b, resid0[:, lane_sets[b]] + mm(comp2[...], xin[:, lane_sets[b]]))
+
+        @pl.when(s == 0)
+        def _():
+            put_resid(b, resid0[:, lane_sets[b]])
+
+        push_resid(b)
+        if b == 0:
+
+            @pl.when(s == 0)
+            def _():
+                push_tags()
+
+    @pl.when(s == 0)
+    def _():
+        prev_copy(s + 1).start()
+        real, imag = unpack(base[:, lane_sets[0]], base[:, lane_sets[1]])
+        sol_ref[0] = real.astype(BF16)
+        sol_ref[1] = imag.astype(BF16)
+        make_owner_tables()
+
+    @pl.when(s > 0)
+    def _():
         for p in range(pieces):
             at = pl.ds(p * rows, rows)
             real, imag = unpack(xin[at, lane_sets[0]], xin[at, lane_sets[1]])
@@ -513,7 +531,7 @@
             return pltpu.VMEM((count, rows, LANES), BF16)
 
         vmem = pl.BlockSpec(memory_space=pltpu.VMEM)
-        anyspace = pl.BlockSpec(memory_space=pl.ANY)
+        anyspace = pl.BlockSpec(memory_space=pltpu.HBM)
         dma = pltpu.SemaphoreType.DMA
         table = pltpu.VMEM((8, LANES), I32)
         smem_table = pltpu.SMEM((8, LANES), I32)
@@ -523,7 +541,7 @@
                 jax.ShapeDtypeStruct((2, interior, cols), BF16),
                 jax.ShapeDtypeStruct((pieces, 2, rows, cols), BF16),
             ),
-            in_specs=[anyspace] * 7,
+            in_specs=[anyspace] * 5 + [pl.BlockSpec(memory_space=pl.ANY), anyspace],
             out_specs=(vmem, vmem),
             scratch_shapes=[
                 pltpu.VMEM((2, interior, cols), BF16),
@@ -577,9 +595,9 @@
                 dma((2,)),
             ],
             compiler_params=pltpu.CompilerParams(
-                collective_id=0, has_side_effects=True, vmem_limit_bytes=60 * 1024 * 1024
+                collective_id=0, has_side_effects=True, vmem_limit_bytes=40 * 1024 * 1024
             ),
-        )(src, inv, cpl, sep, owner_map, piece_count, piece_target[0])
+        )(stay(src), stay(inv), stay(cpl), stay(sep), stay(owner_map), piece_count, stay(piece_target[0]))
         return solved[None, None], trace[None, None]
 
     return jax.shard_map(

time: 140 us -> 132 us (0.943)
  Pallas kernels: 135 us -> 129 us
  local copies, waits for them, and re-layouts: 3.38 us -> 1.42 us
    pallas_call x1, Pallas kernels: 135 us -> 129 us  [body(): pl.pallas_call(functools.partial(sweep_kernel, slabs, fronts, ring), out_...]
    unnamed x2, local copies, waits for them, and re-layouts: 3.38 us -> 1.42 us
where the time goes in v3:
time: 132 us
  Pallas kernels  129 us (98%)
  local copies, waits for them, and re-layouts  1.42 us (1%)
    pallas_call x1, Pallas kernels, body(): pl.pallas_call(functools.partial(sweep_kernel, slabs, fronts, ring), out_...  129 us

profile of v3, /device:TPU:25, one launch (start us, length us, event | category | flops | bytes accessed | tf_op | source)
XLA Modules:
  0.0 131.8 jit_solution(5201191787978044419)
XLA Ops:
  1.3 129.1 %shard_map.86 = (bf16[2,768,128]{2,1,0:T(8,128)(2,1)S(1)}, bf16[24,2,16,128]{3,2,1,0:T(8,128)(2,1)S(1)}) custom-call(bf16[2,768,128]{2,1,0:T(8,128)(2,1)} %bitcast.12, bf16[2,768,768]{2,1,0:T(8,128)(2,1)} %bitcast.9, bf16[2,384,768]{2,1,0:T(8,128)(2,1)} %bitcast.11, bf16[3,2,384,384]{3,2,1,0:T(8,128)(2,1)} %bitcast.10, s32[1,64]{1,0:T(1,128)} %own_hbm.1, ...), custom_call_target="tpu_custom_call" | custom-call | tf_op jit(solution)/shard_map/pallas_call | solution.py:538
  130.4 0.7 copy.12
  131.1 0.7 copy.13

commit v4 on v3

--- a/solution.py
+++ b/solution.py
@@ -13,19 +13,63 @@
 I32 = jnp.int32
 LANES = 128
 HALF = LANES // 2
-BATCHES = 2
+QUARTER = LANES // 4
+BATCHES = 4
+GROUPS = 2
 
 
 def mm(a, b):
     return jnp.dot(a, b, preferred_element_type=F32)
 
 
-def turn(x):
-    return pltpu.roll(x, HALF, 1)
+def turn(x, distance=HALF):
+    return pltpu.roll(x, distance, 1)
 
 
 def iota(shape, axis):
     return lax.broadcasted_iota(I32, shape, axis)
+
+
+def low_half(x):
+    return iota(x.shape, len(x.shape) - 1) < HALF
+
+
+def quarters(a, b, c, d):
+    lane = iota(a.shape, 1)
+    front = jnp.where(lane < QUARTER, a, b)
+    return jnp.where(lane < HALF, front, jnp.where(lane < HALF + QUARTER, c, d))
+
+
+def group_swap(x):
+    left, right = turn(x, LANES - QUARTER), turn(x, QUARTER)
+    return quarters(-left, right, -left, right)
+
+
+def twin_swap(x):
+    moved = turn(x, QUARTER)
+    return quarters(-moved, moved, -moved, moved)
+
+
+def twins(x):
+    turned, low = turn(x), low_half(x)
+    return jnp.where(low, x, turned), jnp.where(low, turned, x)
+
+
+def split_groups(real, imag):
+    left, right = LANES - QUARTER, QUARTER
+    return (
+        quarters(real, turn(imag, right), turn(real, right), turn(imag)),
+        quarters(turn(real), turn(imag, left), turn(real, left), imag),
+    )
+
+
+def join_groups(g0, g1):
+    left, right = LANES - QUARTER, QUARTER
+    g0_left, g1_right = turn(g0, left), turn(g1, right)
+    return (
+        quarters(g0, g0_left, turn(g1), g1_right),
+        quarters(g0_left, turn(g0), g1_right, g1),
+    )
 
 
 def total(mask, value, axis):
@@ -129,6 +173,7 @@
     xs,
     xb,
     xin,
+    xtwin,
     xsep,
     base,
     resid0,
@@ -137,11 +182,15 @@
     out_a,
     recv_a0,
     recv_a1,
+    recv_a2,
+    recv_a3,
     run,
     vals,
     out_b,
     recv_b0,
     recv_b1,
+    recv_b2,
+    recv_b3,
     recv_t,
     home,
     tag_v,
@@ -176,13 +225,15 @@
     slots, sepw = sep2.shape[0], sep2.shape[1]
     pieces = inc.shape[0]
     rows = inc.shape[2]
+    thin = rows // 2
     parts = sepw // rows
     positions = slots * parts
     cap = 2 * fronts
     halves = interior // bnd
     depth = fronts // ring
-    recv_a, recv_b = (recv_a0, recv_a1), (recv_b0, recv_b1)
-    lane_sets = [pl.ds(b * LANES, LANES) for b in range(BATCHES)]
+    recv_a = (recv_a0, recv_a1, recv_a2, recv_a3)
+    recv_b = (recv_b0, recv_b1, recv_b2, recv_b3)
+    lane_sets = [pl.ds(b * LANES, LANES) for b in range(GROUPS)]
 
     f_z, f_x = lax.div(f, ring), lax.rem(f, ring)
     z_of = [lax.rem(f_z + dz, depth) * ring for dz in range(depth)]
@@ -250,8 +301,8 @@
     for copy in sep_loads:
         copy.start()
 
-    zero_block = jnp.zeros((rows, LANES), BF16)
-    run[cap] = jnp.zeros((rows, LANES), F32)
+    zero_block = jnp.zeros((thin, LANES), BF16)
+    run[cap] = jnp.zeros((thin, LANES), F32)
     for b in range(BATCHES):
         rblk[b, pieces] = zero_block
         vals[b, positions] = zero_block
@@ -270,36 +321,29 @@
     bring = pltpu.make_async_copy(leaf_tab, leaf_smem, smem_sem.at[0])
     bring.start()
 
-    def low_half(like):
-        return iota(like.shape, 1) < HALF
-
-    def swap(x):
-        turned = turn(x)
-        return jnp.where(low_half(x), -turned, turned)
-
     load_src.wait()
     for h in range(halves):
         real = src_v[0, pl.ds(h * bnd, bnd), :]
         imag = src_v[1, pl.ds(h * bnd, bnd), :]
         top, low = pl.ds(2 * h * bnd, bnd), pl.ds((2 * h + 1) * bnd, bnd)
-        packed = (
-            jnp.where(low_half(real), real, turn(imag)),
-            jnp.where(low_half(real), turn(real), imag),
-        )
-        for b in range(BATCHES):
-            xs[top, lane_sets[b]] = packed[b]
-            xs[low, lane_sets[b]] = swap(packed[b])
+        packed = split_groups(real, imag)
+        for g in range(GROUPS):
+            xs[top, lane_sets[g]] = packed[g]
+            xs[low, lane_sets[g]] = group_swap(packed[g])
 
     for copy in loads:
         copy.wait()
     base[...] = mm(leaf2[...], xs[...])
-    for b in range(BATCHES):
-        rounded = base[:, lane_sets[b]].astype(BF16)
-        xb[pl.ds(0, interior), lane_sets[b]] = rounded
-        xb[pl.ds(interior, interior), lane_sets[b]] = swap(rounded)
+    for g in range(GROUPS):
+        rounded = base[:, lane_sets[g]].astype(BF16)
+        xb[pl.ds(0, interior), lane_sets[g]] = rounded
+        xb[pl.ds(interior, interior), lane_sets[g]] = group_swap(rounded)
     for copy in cpl_loads:
         copy.wait()
-    resid0[...] = mm(cpl2[...], xb[...])
+    start_resid = mm(cpl2[...], xb[...])
+    for g in range(GROUPS):
+        pair = twins(start_resid[:, g * LANES : (g + 1) * LANES])
+        resid0[2 * g], resid0[2 * g + 1] = pair
     bring.wait()
 
     has_next = jnp.where(s < last, fronts, 0)
@@ -352,8 +396,18 @@
         view = buf.at[pl.ds(0, count)]
         pltpu.make_async_copy(view, view, sem).wait()
 
+    def pack(value, count):
+        block = value.astype(BF16).reshape(count, rows, LANES)
+        upper, lower = block[:, :thin], block[:, thin:]
+        return jnp.where(low_half(upper), upper, lower)
+
+    def spread(block, put):
+        for k, part in enumerate(twins(block)):
+            put(0, k * thin, part)
+            put(1, k * thin, twin_swap(part))
+
     def put_resid(b, resid):
-        rblk[b, pl.ds(0, pieces)] = resid.astype(BF16).reshape(pieces, rows, LANES)
+        rblk[b, pl.ds(0, pieces)] = pack(resid, pieces)
 
     def push_resid(b):
         for i in range(cap):
@@ -374,10 +428,6 @@
         bring.start()
         bring.wait()
 
-    def unpack(b0, b1):
-        first = low_half(b0)
-        return jnp.where(first, b0, turn(b1)), jnp.where(first, turn(b0), b1)
-
     tag_recv[f] = tag_v[...]
 
     @pl.when(s > 0)
@@ -405,14 +455,16 @@
         def _():
             await_bytes(recv_b[b], cap, b_arrive.at[b])
             for p in range(pieces):
-                block = recv_b[b][prev_smem[1, p]]
-                xin[pl.ds(p * rows, rows), lane_sets[b]] = block
-                xin[pl.ds(bnd + p * rows, rows), lane_sets[b]] = swap(block)
-            put_resid(b, resid0[:, lane_sets[b]] + mm(comp2[...], xin[:, lane_sets[b]]))
+
+                def put(which, offset, part):
+                    xtwin[b, pl.ds(which * bnd + p * rows + offset, thin), :] = part
+
+                spread(recv_b[b][prev_smem[1, p]], put)
+            put_resid(b, resid0[b] + mm(comp2[...], xtwin[b]))
 
         @pl.when(s == 0)
         def _():
-            put_resid(b, resid0[:, lane_sets[b]])
+            put_resid(b, resid0[b])
 
         push_resid(b)
         if b == 0:
@@ -424,42 +476,41 @@
     @pl.when(s == 0)
     def _():
         prev_copy(s + 1).start()
-        real, imag = unpack(base[:, lane_sets[0]], base[:, lane_sets[1]])
-        sol_ref[0] = real.astype(BF16)
-        sol_ref[1] = imag.astype(BF16)
         make_owner_tables()
 
     @pl.when(s > 0)
     def _():
-        for p in range(pieces):
-            at = pl.ds(p * rows, rows)
-            real, imag = unpack(xin[at, lane_sets[0]], xin[at, lane_sets[1]])
-            inc[p, 0] = real
-            inc[p, 1] = imag
+        for g in range(GROUPS):
+            even, odd = xtwin[2 * g], xtwin[2 * g + 1]
+            xin[:, lane_sets[g]] = jnp.where(low_half(even), even, odd)
+        real, imag = join_groups(xin[pl.ds(0, bnd), lane_sets[0]], xin[pl.ds(0, bnd), lane_sets[1]])
+        inc[:, 0] = real.reshape(pieces, rows, LANES)
+        inc[:, 1] = imag.reshape(pieces, rows, LANES)
         home_copy(s - 1).start()
-        full = base[...] + mm(leaf2[:, pl.ds(0, 2 * bnd)], xin[...])
-        real, imag = unpack(full[:, :LANES], full[:, LANES:])
-        sol_ref[0] = real.astype(BF16)
-        sol_ref[1] = imag.astype(BF16)
+
+    def put_solution(full):
+        full = full.astype(BF16)
+        sol_ref[0], sol_ref[1] = join_groups(full[:, :LANES], full[:, LANES:])
 
     for copy in sep_loads:
         copy.wait()
 
     for b in range(BATCHES):
         await_bytes(recv_a[b], cap - 2, a_arrive.at[b])
-        running = jnp.zeros((rows, LANES), F32)
+        running = jnp.zeros((thin, LANES), F32)
         for i in range(cap):
             block = recv_a[b][own_smem[0, i]].astype(F32)
             running = jnp.where(own_smem[1, i] > 0, running, 0.0) + block
             run[i] = running
         for m in range(slots):
             for q in range(parts):
-                block = run[own_smem[2, m * parts + q]].astype(BF16)
-                xsep[m, pl.ds(q * rows, rows), :] = block
-                xsep[m, pl.ds(sepw + q * rows, rows), :] = swap(block)
+
+                def put(which, offset, part):
+                    xsep[m, pl.ds(which * sepw + q * rows + offset, thin), :] = part
+
+                spread(run[own_smem[2, m * parts + q]].astype(BF16), put)
         for m in range(slots):
-            value = mm(sep2[m], xsep[m]).astype(BF16)
-            vals[b, pl.ds(m * parts, parts)] = value.reshape(parts, rows, LANES)
+            vals[b, pl.ds(m * parts, parts)] = pack(mm(sep2[m], xsep[m]), parts)
         for i in range(cap):
             out_b[b, i] = vals[b, own_smem[3, i]]
 
@@ -477,6 +528,14 @@
             for k in range(2):
                 recv_t[b, 2 * f + k] = out_b[b, 2 * f + k]
 
+    @pl.when(s == 0)
+    def _():
+        put_solution(base[...])
+
+    @pl.when(s > 0)
+    def _():
+        put_solution(base[...] + mm(leaf2[:, pl.ds(0, 2 * bnd)], xin[...]))
+
     @pl.when(s < last)
     def _():
         home_copy(s).wait_recv()
@@ -491,9 +550,15 @@
             await_bytes(recv_t.at[b], cap - 2, t_arrive.at[b])
         for p in range(pieces):
             at = leaf_smem[1, p]
-            real, imag = unpack(recv_t[0, at], recv_t[1, at])
-            trace_ref[p, 0] = real
-            trace_ref[p, 1] = imag
+            pairs = [twins(recv_t[b, at]) for b in range(BATCHES)]
+            for k in range(2):
+                low = low_half(pairs[0][k])
+                real, imag = join_groups(
+                    jnp.where(low, pairs[0][k], pairs[1][k]),
+                    jnp.where(low, pairs[2][k], pairs[3][k]),
+                )
+                trace_ref[p, 0, pl.ds(k * thin, thin), :] = real
+                trace_ref[p, 1, pl.ds(k * thin, thin), :] = imag
         for b in range(BATCHES):
             await_bytes(out_b.at[b], cap - 2, b_send.at[b])
 
@@ -525,10 +590,10 @@
         halves = interior // bnd
 
         def blocks(count):
-            return pltpu.VMEM((BATCHES, count, rows, LANES), BF16)
+            return pltpu.VMEM((BATCHES, count, rows // 2, LANES), BF16)
 
         def single(count):
-            return pltpu.VMEM((count, rows, LANES), BF16)
+            return pltpu.VMEM((count, rows // 2, LANES), BF16)
 
         vmem = pl.BlockSpec(memory_space=pltpu.VMEM)
         anyspace = pl.BlockSpec(memory_space=pltpu.HBM)
@@ -555,17 +620,22 @@
                 pltpu.VMEM((2 * interior, 2 * cols), BF16),
                 pltpu.VMEM((2 * interior, 2 * cols), BF16),
                 pltpu.VMEM((2 * bnd, 2 * cols), BF16),
+                pltpu.VMEM((BATCHES, 2 * bnd, LANES), BF16),
                 pltpu.VMEM((slots, 2 * sepw, LANES), BF16),
                 pltpu.VMEM((interior, 2 * cols), F32),
-                pltpu.VMEM((bnd, 2 * cols), F32),
+                pltpu.VMEM((BATCHES, bnd, LANES), F32),
                 blocks(pieces + 1),
                 pltpu.VMEM((pieces, 2, rows, cols), BF16),
                 blocks(cap),
                 single(cap),
                 single(cap),
-                pltpu.VMEM((cap + 1, rows, LANES), F32),
+                single(cap),
+                single(cap),
+                pltpu.VMEM((cap + 1, rows // 2, LANES), F32),
                 blocks(positions + 1),
                 blocks(cap),
+                single(cap + 1),
+                single(cap + 1),
                 single(cap + 1),
                 single(cap + 1),
                 blocks(cap + 1),

time: 132 us -> 122 us (0.924)
  Pallas kernels: 129 us -> 119 us
    pallas_call x1, Pallas kernels: 129 us -> 119 us  [body(): pl.pallas_call(functools.partial(sweep_kernel, slabs, fronts, ring), out_...]
where the time goes in v4:
time: 122 us
  Pallas kernels  119 us (98%)
  local copies, waits for them, and re-layouts  1.42 us (1%)
  between operations  1.29 us (1%)
    pallas_call x1, Pallas kernels, body(): pl.pallas_call(functools.partial(sweep_kernel, slabs, fronts, ring), out_...  119 us

profile of v4, /device:TPU:25, one launch (start us, length us, event | category | flops | bytes accessed | tf_op | source)
XLA Modules:
  0.0 121.7 jit_solution(8370865907658523636)
XLA Ops:
  1.3 119.0 %shard_map.86 = (bf16[2,768,128]{2,1,0:T(8,128)(2,1)S(1)}, bf16[24,2,16,128]{3,2,1,0:T(8,128)(2,1)S(1)}) custom-call(bf16[2,768,128]{2,1,0:T(8,128)(2,1)} %bitcast.12, bf16[2,768,768]{2,1,0:T(8,128)(2,1)} %bitcast.9, bf16[2,384,768]{2,1,0:T(8,128)(2,1)} %bitcast.11, bf16[3,2,384,384]{3,2,1,0:T(8,128)(2,1)} %bitcast.10, s32[1,64]{1,0:T(1,128)} %own_hbm.1, ...), custom_call_target="tpu_custom_call" | custom-call | tf_op jit(solution)/shard_map/pallas_call | solution.py:603
  120.3 0.7 copy.12
  121.0 0.7 copy.13

commit v5 on v4

--- a/solution.py
+++ b/solution.py
@@ -309,7 +309,7 @@
         recv_b[b][cap] = zero_block
         recv_t[b, cap] = zero_block
 
-    for copy in smalls:
+    for copy in smalls + [load_src]:
         copy.wait()
     out_src, tag, back = leaf_tables(
         own_v[...], tgt_v[...], cnt_s[0, 0], parts, positions, fronts
@@ -321,7 +321,6 @@
     bring = pltpu.make_async_copy(leaf_tab, leaf_smem, smem_sem.at[0])
     bring.start()
 
-    load_src.wait()
     for h in range(halves):
         real = src_v[0, pl.ds(h * bnd, bnd), :]
         imag = src_v[1, pl.ds(h * bnd, bnd), :]
@@ -430,10 +429,10 @@
 
     tag_recv[f] = tag_v[...]
 
+    push_tags()
+
     @pl.when(s > 0)
     def _():
-        push_tags()
-
         @pl.when(s < last)
         def _():
             prev_copy(s + 1).start()
@@ -467,12 +466,6 @@
             put_resid(b, resid0[b])
 
         push_resid(b)
-        if b == 0:
-
-            @pl.when(s == 0)
-            def _():
-                push_tags()
-
     @pl.when(s == 0)
     def _():
         prev_copy(s + 1).start()

time: 122 us -> 120 us (0.984)
    pallas_call x1, Pallas kernels: 119 us -> 118 us  [body(): pl.pallas_call(functools.partial(sweep_kernel, slabs, fronts, ring), out_...]
where the time goes in v5:
time: 120 us
  Pallas kernels  118 us (98%)
  local copies, waits for them, and re-layouts  1.42 us (1%)
  between operations  1.29 us (1%)
    pallas_call x1, Pallas kernels, body(): pl.pallas_call(functools.partial(sweep_kernel, slabs, fronts, ring), out_...  118 us

profile of v5, /device:TPU:25, one launch (start us, length us, event | category | flops | bytes accessed | tf_op | source)
XLA Modules:
  0.0 120.2 jit_solution(10056081522841627876)
XLA Ops:
  1.3 117.5 %shard_map.86 = (bf16[2,768,128]{2,1,0:T(8,128)(2,1)S(1)}, bf16[24,2,16,128]{3,2,1,0:T(8,128)(2,1)S(1)}) custom-call(bf16[2,768,128]{2,1,0:T(8,128)(2,1)} %bitcast.12, bf16[2,768,768]{2,1,0:T(8,128)(2,1)} %bitcast.9, bf16[2,384,768]{2,1,0:T(8,128)(2,1)} %bitcast.11, bf16[3,2,384,384]{3,2,1,0:T(8,128)(2,1)} %bitcast.10, s32[1,64]{1,0:T(1,128)} %own_hbm.1, ...), custom_call_target="tpu_custom_call" | custom-call | tf_op jit(solution)/shard_map/pallas_call | solution.py:596
  118.8 0.7 copy.12
  119.6 0.7 copy.13

commit v6 on v5

--- a/solution.py
+++ b/solution.py
@@ -42,12 +42,12 @@
 
 def group_swap(x):
     left, right = turn(x, LANES - QUARTER), turn(x, QUARTER)
-    return quarters(-left, right, -left, right)
+    return jnp.where(iota(x.shape, 1) % HALF < QUARTER, -left, right)
 
 
 def twin_swap(x):
     moved = turn(x, QUARTER)
-    return quarters(-moved, moved, -moved, moved)
+    return jnp.where(iota(x.shape, 1) % HALF < QUARTER, -moved, moved)
 
 
 def twins(x):

time: 120 us -> 120 us (level)
  no operation moved by 1% of the time
where the time goes in v6:
time: 120 us
  Pallas kernels  117 us (98%)
  local copies, waits for them, and re-layouts  1.42 us (1%)
  between operations  1.29 us (1%)
    pallas_call x1, Pallas kernels, body(): pl.pallas_call(functools.partial(sweep_kernel, slabs, fronts, ring), out_...  117 us

profile of v6, /device:TPU:25, one launch (start us, length us, event | category | flops | bytes accessed | tf_op | source)
XLA Modules:
  0.0 119.9 jit_solution(16570539093823111054)
XLA Ops:
  1.3 117.2 %shard_map.86 = (bf16[2,768,128]{2,1,0:T(8,128)(2,1)S(1)}, bf16[24,2,16,128]{3,2,1,0:T(8,128)(2,1)S(1)}) custom-call(bf16[2,768,128]{2,1,0:T(8,128)(2,1)} %bitcast.12, bf16[2,768,768]{2,1,0:T(8,128)(2,1)} %bitcast.9, bf16[2,384,768]{2,1,0:T(8,128)(2,1)} %bitcast.11, bf16[3,2,384,384]{3,2,1,0:T(8,128)(2,1)} %bitcast.10, s32[1,64]{1,0:T(1,128)} %own_hbm.1, ...), custom_call_target="tpu_custom_call" | custom-call | tf_op jit(solution)/shard_map/pallas_call | solution.py:596
  118.5 0.7 copy.12
  119.2 0.7 copy.13
